TPU v7x, 256 devices: a whole 4x4x8 slice. The times are simulated.
256 devices in a mesh: apa: 32 (over x_hi, z, core), chan: 8 (over x_lo, y).
Axes of the slice: x: 4 (x_hi: 2, x_lo: 2; x = x_hi * 2 + x_lo), y: 4, z: 8, core: 2. Of those that a mesh axis runs over, the one named last changes fastest.
Arguments:
- frames: bfloat16 [32, 2560, 256], P('apa', 'chan'), may hold values from -6 to 6
- link_to_wire: int32 [32, 2560], P('apa'), may hold values from 0 to 2559, each once within a row
- neighbours: int32 [32, 2], P('apa'), may hold values from -1 to 31, as said below
- kernel: float32 [2, 128, 2816], P(None, 'chan'), may hold values from -6 to 6
- wide_filter: float32 [128], replicated, may hold values from 0.3 to 1
- tight_filter: float32 [128], replicated, may hold values from 0.05 to 0.5
- roi_mask: int32 [32, 160, 4], P('apa', 'chan'), may hold values 0 or 1
Outputs:
- deconvolved: float32 [32, 2560, 256], P('apa', 'chan')
Inputs may be any that keep to these rules, and one draw needn't show every extreme that they name: `link_to_wire`: each row names every channel once. `neighbours`: the 32 APAs form one chain along the detector: column 0 names the APA before, column 1 the APA after, -1 at the two ends of the chain; every named APA lies on the same index of apa as the naming APA or on an adjacent one.
All inputs are finite; a program needn't handle non-finite values. No bound on the sum of `roi_mask` on one device may be relied on, other than what follows from the above.
Results may differ from a plain program's by a relative error of at most 0.0023.
Values may be sent and summed in bfloat16 or wider, within the bound.
A program may use at most 128 MiB of HBM per device.

v0:
```python
import math

import jax
import jax.numpy as jnp
import numpy as np
from jax import lax
from jax.experimental import pallas as pl
from jax.experimental.pallas import tpu as pltpu
from jax.sharding import PartitionSpec as P

PU = 800
PV = 800
PW = 960
HALO = 128
BC = 16
BT = 64
CHANNELS = 2560
TICKS = 256
FREQS = 128

CHAN = 8
SHARE = CHANNELS // CHAN
PAD = 384
KB = FREQS // CHAN
ROWS = 2 * KB
RADIX = 8
NU = PU // RADIX
PE = PW + 2 * HALO
NW = PE // RADIX
LINKS = CHAN * PAD
OUTS = SHARE // RADIX

MESH = pl.DeviceIdType.MESH
NT = (((1,), (1,)), ((), ()))
f32 = jnp.float32
bf16 = jnp.bfloat16


def halves(table):
    high = table.astype(bf16)
    low = (table - high.astype(np.float64)).astype(bf16)
    return high, low


def tick_rows():
    row = np.arange(2 * FREQS)
    k = row // ROWS * KB + row % KB
    return k, row % ROWS // KB


def forward_ticks():
    k, z = tick_rows()
    angle = 2.0 * math.pi / TICKS * (k[:, None] * np.arange(TICKS)[None, :] % TICKS)
    return np.where(z[:, None] == 0, np.cos(angle), -np.sin(angle)).astype(bf16)


def inverse_ticks():
    k, z = tick_rows()
    angle = 2.0 * math.pi / TICKS * (k[:, None] * np.arange(TICKS)[None, :] % TICKS)
    weight = np.where(k == 0, 1.0, 2.0)[:, None] / TICKS
    return np.stack(halves(np.where(z[:, None] == 0, np.cos(angle), -np.sin(angle)) * weight))


def spread_filters():
    k, _ = tick_rows()
    return (np.arange(FREQS)[:, None] == k[None, :]).astype(np.float32)


def dense(length, width, scale=1.0):
    index = np.arange(length)
    angle = 2.0 * math.pi / length * (index[:, None] * index[None, :] % length)
    table = np.zeros((width, 2 * width))
    table[:length, :length] = np.cos(angle) * scale
    table[:length, width : width + length] = np.sin(angle) * scale
    return table


def forward_dense(length, width):
    high, low = halves(dense(length, width))
    return np.concatenate([high, high, low], axis=0)


def inverse_dense(length, width, period, first, count, lead, rows):
    table = np.zeros((rows, 2 * width))
    table[lead : lead + count] = dense(length, width, 1.0 / period)[first : first + count]
    return np.stack(halves(table))


def twiddles(length, width, period):
    angle = 2.0 * math.pi / period * (np.arange(RADIX)[:, None] * np.arange(length)[None, :])
    table = np.zeros((2, RADIX, 1, width), np.float32)
    table[0, :, 0, :length] = np.cos(angle)
    table[1, :, 0, :length] = np.sin(angle)
    return table


def rim_places():
    lane = np.arange(2 * HALO)
    place = np.where(lane < HALO, lane // RADIX, (HALO + PW) // RADIX + (lane - HALO) // RADIX)
    return (np.arange(256)[:, None] == place[None, :]).astype(np.float32).astype(bf16)


def mask_rows():
    return (np.arange(OUTS)[:, None] // (BC // RADIX) == np.arange(SHARE // BC)[None, :]).astype(np.float32)


def mask_columns():
    return (np.arange(TICKS // BT)[:, None] == np.arange(TICKS)[None, :] // BT).astype(np.float32)


def split(value):
    high = value.astype(bf16)
    return high, (value - high.astype(f32)).astype(bf16)


def mul(left, right):
    return jnp.dot(left, right, preferred_element_type=f32)


def mul_nt(left, right):
    return lax.dot_general(left, right, NT, preferred_element_type=f32)


def four(values, sign):
    (ar, ai), (br, bi), (cr, ci), (dr, di) = values
    s0r, s0i, s1r, s1i = ar + cr, ai + ci, ar - cr, ai - ci
    s2r, s2i, s3r, s3i = br + dr, bi + di, br - dr, bi - di
    if sign > 0:
        tr, ti = -s3i, s3r
    else:
        tr, ti = s3i, -s3r
    return [(s0r + s2r, s0i + s2i), (s1r + tr, s1i + ti), (s0r - s2r, s0i - s2i), (s1r - tr, s1i - ti)]


def eight(values, sign):
    even = four(values[0::2], sign)
    odd = four(values[1::2], sign)
    root = math.sqrt(0.5)
    r, i = odd[1]
    odd[1] = ((r - sign * i) * root, (i + sign * r) * root)
    r, i = odd[2]
    odd[2] = (-i, r) if sign > 0 else (i, -r)
    r, i = odd[3]
    odd[3] = ((-r - sign * i) * root, (sign * r - i) * root)
    first = [(a + c, b + d) for (a, b), (c, d) in zip(even, odd)]
    second = [(a - c, b - d) for (a, b), (c, d) in zip(even, odd)]
    return first + second


def channel_product(product, kern, twiddle, width):
    values = []
    for c in range(RADIX):
        re = product[c * ROWS : c * ROWS + KB]
        im = product[c * ROWS + KB : (c + 1) * ROWS]
        yr = re[:, :width] + im[:, width:]
        yi = im[:, :width] - re[:, width:]
        if c > 0:
            tc, ts = twiddle[0, c], twiddle[1, c]
            yr, yi = yr * tc + yi * ts, yi * tc - yr * ts
        values.append((yr, yi))
    values = eight(values, -1)
    values = [
        (r * kern[m, 0] - i * kern[m, 1], r * kern[m, 1] + i * kern[m, 0]) for m, (r, i) in enumerate(values)
    ]
    values = eight(values, 1)
    rows = []
    for c, (r, i) in enumerate(values):
        if c > 0:
            tc, ts = twiddle[0, c], twiddle[1, c]
            r, i = r * tc - i * ts, i * tc + r * ts
        rows.append(jnp.concatenate([r, -i], axis=1))
        rows.append(jnp.concatenate([i, r], axis=1))
    return jnp.concatenate(rows, axis=0)


def inverse_product(table, value):
    high, low = split(value)
    return mul_nt(table[0], high) + mul_nt(table[1], high) + mul_nt(table[0], low)


def kernel_window(kern, part, start, length, width):
    base = start // 128 * 128
    span = -(-(start - base + length) // 128) * 128
    span = max(span, width)
    piece = kern[part, :, base : base + span]
    if start > base:
        piece = pltpu.roll(piece, span - (start - base), axis=1)
    return piece[:, :width]


INPUTS = 17


def body_kernel(apas, near, *refs):
    hbm = refs[:INPUTS]
    out = refs[INPUTS]
    local = refs[INPUTS + 1 : 2 * INPUTS + 1]
    (tx1, rx1, tx2, rx2, txh, rxh, onehot, edge, masks, big, small, kern_u, kern_v, kern_w, result) = refs[
        2 * INPUTS + 1 : 2 * INPUTS + 16
    ]
    in_sem, send1, recv1, send2, recv2, sendh, recvh, out_sem = refs[2 * INPUTS + 16 :]
    (frames, ticks, links, kern, wide, tight, roi, fwd_u, fwd_w, inv_u, inv_v, inv_w, tw_u, tw_w, rim, back, expand) = local

    me = lax.axis_index("chan")
    apa = lax.axis_index("apa")
    after = lax.rem(apa + 1, apas)
    before = lax.rem(apa + apas - 1, apas)

    loads = [pltpu.make_async_copy(hbm[i], local[i], in_sem.at[i]) for i in range(INPUTS)]
    for load in loads:
        load.start()

    barrier = pltpu.get_barrier_semaphore()
    for step in range(1, CHAN):
        pl.semaphore_signal(barrier, inc=1, device_id={"chan": lax.rem(me + step, CHAN)}, device_id_type=MESH)
    pl.semaphore_signal(barrier, inc=1, device_id={"apa": after}, device_id_type=MESH)
    pl.semaphore_signal(barrier, inc=1, device_id={"apa": before}, device_id_type=MESH)

    loads[0].wait()
    loads[1].wait()
    padded = jnp.concatenate([frames[0], jnp.zeros((PAD - SHARE, TICKS), bf16)], axis=0)
    tx1[...] = mul_nt(ticks[...], padded).reshape(CHAN, ROWS, PAD)

    pl.semaphore_wait(barrier, CHAN + 1)

    def first_copy(step):
        dest = lax.rem(me + step, CHAN)
        return pltpu.make_async_remote_copy(
            src_ref=tx1.at[dest],
            dst_ref=rx1.at[me],
            send_sem=send1.at[dest],
            recv_sem=recv1.at[me],
            device_id={"chan": dest},
            device_id_type=MESH,
        )

    for step in range(1, CHAN):
        first_copy(step).start()
    rx1[me] = tx1[me]

    loads[2].wait()
    for s in range(CHAN):
        wire = links[:, s * SHARE : (s + 1) * SHARE]
        wire = jnp.concatenate([wire, jnp.full((1, PAD - SHARE), -8, jnp.int32)], axis=1)
        group = lax.shift_right_arithmetic(wire, 3)
        rest = lax.bitwise_and(wire, 7)
        place = group + jnp.where(wire >= PU + PV, 72, jnp.where(wire >= PU, 28, 0))
        row = lax.broadcasted_iota(jnp.int32, (512, PAD), 0)
        onehot[:, s * PAD : (s + 1) * PAD] = jnp.where(row == place, 1.0, 0.0).astype(bf16)
        row = lax.broadcasted_iota(jnp.int32, (256, PAD), 0)
        spot = row + jnp.where(row >= HALO, CHANNELS - 2 * HALO, PU + PV)
        edge[:, s * PAD : (s + 1) * PAD] = jnp.where(spot == wire, 1.0, 0.0).astype(bf16)
        for h in range(RADIX):
            here = jnp.where((rest == h) & (wire >= 0), 1.0, 0.0)
            masks[s, h] = jnp.broadcast_to(here, (16, PAD)).astype(bf16)

    loads[3].wait()
    for m in range(RADIX):
        for part in range(2):
            kern_u[m, part] = kernel_window(kern, part, NU * m, NU, 128)
            kern_v[m, part] = kernel_window(kern, part, PU + NU * m, NU, 128)
            kern_w[m, part] = kernel_window(kern, part, PU + PV + NW * m, NW, 256)

    for load in loads[4:]:
        load.wait()
    gains = jnp.concatenate([wide[...], tight[...], jnp.zeros((6, FREQS), f32)], axis=0)
    gains = jnp.dot(gains, expand[0:FREQS], precision=lax.Precision.HIGHEST, preferred_element_type=f32)
    inside = roi[0].astype(f32)
    row_index = lax.broadcasted_iota(jnp.int32, (OUTS, SHARE // BC), 0) // (BC // RADIX)
    col_index = lax.broadcasted_iota(jnp.int32, (OUTS, SHARE // BC), 1)
    pick = jnp.where(row_index == col_index, 1.0, 0.0)
    inside = mul(pick, inside)
    row_index = lax.broadcasted_iota(jnp.int32, (TICKS // BT, TICKS), 0)
    col_index = lax.broadcasted_iota(jnp.int32, (TICKS // BT, TICKS), 1) // BT
    inside = mul(inside, jnp.where(row_index == col_index, 1.0, 0.0))

    for step in range(1, CHAN):
        source = lax.rem(me + step, CHAN)
        pltpu.make_async_remote_copy(
            src_ref=tx1.at[source],
            dst_ref=rx1.at[source],
            send_sem=send1.at[source],
            recv_sem=recv1.at[source],
            device_id={"chan": source},
            device_id_type=MESH,
        ).wait_recv()
    for s in range(CHAN):
        lanes = slice(s * PAD, (s + 1) * PAD)
        high, low = split(rx1[s])
        small[0:ROWS, lanes] = high
        small[ROWS : 2 * ROWS, lanes] = low
        for h in range(RADIX):
            mask = jnp.concatenate([masks[s, h], masks[s, h]], axis=0)
            big[h * ROWS : (h + 1) * ROWS, lanes] = high * mask
            big[256 + h * ROWS : 256 + (h + 1) * ROWS, lanes] = low * mask

    bands = mul_nt(small[...], edge[...])
    first_band = bands[:, :HALO]
    last_band = bands[:, HALO:]
    lower = near[0, 0]
    upper = near[0, 1]
    none = jnp.zeros_like(first_band)
    to_after = jnp.where(upper == after, last_band, jnp.where(lower == after, first_band, none))
    to_before = jnp.where(lower == before, first_band, jnp.where(upper == before, last_band, none))
    txh[0] = to_after.astype(bf16)
    txh[1] = to_before.astype(bf16)

    def edge_copy(way):
        return pltpu.make_async_remote_copy(
            src_ref=txh.at[way],
            dst_ref=rxh.at[way],
            send_sem=sendh.at[way],
            recv_sem=recvh.at[way],
            device_id={"apa": after if way == 0 else before},
            device_id_type=MESH,
        )

    edge_copy(0).start()
    edge_copy(1).start()

    placed = mul_nt(big[...], onehot[...])

    def second_copy(dest):
        return pltpu.make_async_remote_copy(
            src_ref=tx2.at[dest],
            dst_ref=rx2.at[me],
            send_sem=send2.at[dest],
            recv_sem=recv2.at[me],
            device_id={"chan": dest},
            device_id_type=MESH,
        )

    def send_on(dests):
        for dest in dests:

            @pl.when(me != dest)
            def _():
                second_copy(dest).start()

            @pl.when(me == dest)
            def _():
                rx2[dest] = tx2[dest]

    def plane(lanes, fwd, kern_part, twiddle, table, width):
        high = placed[0:256, lanes].astype(bf16)
        low = placed[256:512, lanes].astype(bf16)
        product = mul(jnp.concatenate([high, low, high], axis=1), fwd[...])
        return inverse_product(table, channel_product(product, kern_part, twiddle, width))

    part_u = plane(slice(0, 128), fwd_u, kern_u, tw_u, inv_u, 128)
    part_v = plane(slice(128, 256), fwd_u, kern_v, tw_u, inv_v, 128)
    tx2[0] = part_u[0:40]
    tx2[1] = part_u[40:80]
    tx2[2, 0:16] = part_u[80:96]
    tx2[2, 16:24] = part_u[96:104] + part_v[0:8]
    tx2[2, 24:40] = part_v[8:24]
    tx2[3] = part_v[24:64]
    tx2[4] = part_v[64:104]
    send_on(range(0, 5))

    edge_copy(0).wait_recv()
    edge_copy(1).wait_recv()
    from_before = rxh[0].astype(f32)
    from_after = rxh[1].astype(f32)
    blank = jnp.zeros_like(from_before)
    rim_low = jnp.where(lower == before, from_before, jnp.where(lower == after, from_after, blank))
    rim_up = jnp.where(upper == after, from_after, jnp.where(upper == before, from_before, blank))
    rims = jnp.concatenate([rim_low, rim_up], axis=1)
    lane = lax.bitwise_and(lax.broadcasted_iota(jnp.int32, (ROWS, 2 * HALO), 1), RADIX - 1)
    spread = [
        jnp.where(lane == h, rims[part * ROWS : (part + 1) * ROWS], 0.0) for part in range(2) for h in range(RADIX)
    ]
    rim_part = mul_nt(jnp.concatenate(spread, axis=0).astype(bf16), rim[...])
    full = placed[:, 256:512] + rim_part
    high = full[0:256].astype(bf16)
    low = full[256:512].astype(bf16)
    product = mul(jnp.concatenate([high, low, high], axis=1), fwd_w[...])
    part_w = inverse_product(inv_w, channel_product(product, kern_w, tw_w, 256))
    tx2[5] = part_w[0:40]
    tx2[6] = part_w[40:80]
    tx2[7] = part_w[80:120]
    send_on(range(5, 8))

    for step in range(1, CHAN):
        source = lax.rem(me + step, CHAN)
        pltpu.make_async_remote_copy(
            src_ref=tx2.at[source],
            dst_ref=rx2.at[source],
            send_sem=send2.at[source],
            recv_sem=recv2.at[source],
            device_id={"chan": source},
            device_id_type=MESH,
        ).wait_recv()

    block = lax.broadcasted_iota(jnp.int32, (OUTS, 128), 1) // ROWS
    columns = []
    for side in range(2):
        for c in range(RADIX):
            acc = None
            for q in range(4):
                piece = rx2[4 * side + q, :, c // 4 * 128 : (c // 4 + 1) * 128]
                turn = (q - c % 4) % 4 * ROWS
                if turn:
                    piece = pltpu.roll(piece, turn, axis=1)
                acc = piece if acc is None else jnp.where(block == q, piece, acc)
            columns.append(acc)
    gathered = jnp.concatenate(
        [jnp.concatenate(columns[:RADIX], axis=0), jnp.concatenate(columns[RADIX:], axis=0)], axis=1
    )

    def signal(gain):
        high, low = split(gathered * gain)
        return mul(high, back[0]) + mul(low, back[0]) + mul(high, back[1])

    wide_signal = signal(gains[0:1])
    tight_signal = signal(gains[1:2])
    for c in range(RADIX):
        rows = slice(c * OUTS, (c + 1) * OUTS)
        chosen = jnp.where(inside > 0.5, wide_signal[rows], tight_signal[rows])
        for side in range(2):
            result[side, pl.ds(c, OUTS, stride=RADIX), :] = chosen[:, side * 128 : (side + 1) * 128]
    stores = [
        pltpu.make_async_copy(result.at[side], out.at[0, :, pl.ds(side * 128, 128)], out_sem.at[side])
        for side in range(2)
    ]
    for store in stores:
        store.start()
    for store in stores:
        store.wait()

    for step in range(1, CHAN):
        first_copy(step).wait_send()
        second_copy(lax.rem(me + step, CHAN)).wait_send()
    edge_copy(0).wait_send()
    edge_copy(1).wait_send()


def body(frames, links, near, kern, wide, tight, roi):
    apas = lax.axis_size("apa")
    arrays = [
        frames,
        jnp.asarray(forward_ticks()),
        links,
        kern,
        wide.reshape(1, FREQS),
        tight.reshape(1, FREQS),
        roi,
        jnp.asarray(forward_dense(NU, 128)),
        jnp.asarray(forward_dense(NW, 256)),
        jnp.asarray(inverse_dense(NU, 128, PU, 0, NU, 0, 104)),
        jnp.asarray(inverse_dense(NU, 128, PV, 0, NU, 4, 104)),
        jnp.asarray(inverse_dense(NW, 256, PE, HALO // RADIX, PW // RADIX, 0, 120)),
        jnp.asarray(twiddles(NU, 128, PU)),
        jnp.asarray(twiddles(NW, 256, PE)),
        jnp.asarray(rim_places()),
        jnp.asarray(inverse_ticks()),
        jnp.asarray(spread_filters()),
    ]
    scratch = [pltpu.VMEM(a.shape, a.dtype) for a in arrays]
    scratch += [
        pltpu.VMEM((CHAN, ROWS, PAD), f32),
        pltpu.VMEM((CHAN, ROWS, PAD), f32),
        pltpu.VMEM((CHAN, OUTS, 256), f32),
        pltpu.VMEM((CHAN, OUTS, 256), f32),
        pltpu.VMEM((2, 2 * ROWS, HALO), bf16),
        pltpu.VMEM((2, 2 * ROWS, HALO), bf16),
        pltpu.VMEM((512, LINKS), bf16),
        pltpu.VMEM((256, LINKS), bf16),
        pltpu.VMEM((CHAN, RADIX, 16, PAD), bf16),
        pltpu.VMEM((512, LINKS), bf16),
        pltpu.VMEM((2 * ROWS, LINKS), bf16),
        pltpu.VMEM((RADIX, 2, KB, 128), f32),
        pltpu.VMEM((RADIX, 2, KB, 128), f32),
        pltpu.VMEM((RADIX, 2, KB, 256), f32),
        pltpu.VMEM((2, SHARE, 128), f32),
        pltpu.SemaphoreType.DMA((INPUTS,)),
        pltpu.SemaphoreType.DMA((CHAN,)),
        pltpu.SemaphoreType.DMA((CHAN,)),
        pltpu.SemaphoreType.DMA((CHAN,)),
        pltpu.SemaphoreType.DMA((CHAN,)),
        pltpu.SemaphoreType.DMA((2,)),
        pltpu.SemaphoreType.DMA((2,)),
        pltpu.SemaphoreType.DMA((2,)),
    ]

    def kernel(near_ref, *refs):
        body_kernel(apas, near_ref, *refs)

    return pl.pallas_call(
        kernel,
        out_shape=jax.ShapeDtypeStruct(frames.shape, f32),
        in_specs=[pl.BlockSpec(memory_space=pltpu.SMEM)] + [pl.BlockSpec(memory_space=pl.ANY)] * len(arrays),
        out_specs=pl.BlockSpec(memory_space=pl.ANY),
        scratch_shapes=scratch,
        compiler_params=pltpu.CompilerParams(
            collective_id=0, has_side_effects=True, vmem_limit_bytes=48 * 1024 * 1024
        ),
    )(near, *arrays)


def solution(mesh):
    placed = (
        P("apa", "chan", None),
        P("apa", None),
        P("apa", None),
        P(None, "chan", None),
        P(),
        P(),
        P("apa", "chan", None),
    )
    return jax.shard_map(body, mesh=mesh, in_specs=placed, out_specs=P("apa", "chan", None), check_vma=False)
```

profile of v0, /device:TPU:10, one launch (start us, length us, event | category | flops | bytes accessed | tf_op | source)
XLA Modules:
  0.0 40.5 jit_solution(1677242251694263142)
XLA Ops:
  0.0 0.0 copy-start.11
  0.0 0.0 copy-start.12
  0.0 0.0 copy-start.14
  0.0 0.0 copy-start.15
  0.0 0.0 copy-start.16
  0.0 0.8 %copy.19.refs_6_ = s32[1,20,4]{2,1,0:T(8,128)S(1)} copy(s32[1,20,4]{1,2,0:T(4,128)} %param.24) | data formatting | bytes 640 | tf_op args[6]
  0.9 0.0 copy-done.11
  0.9 0.0 copy-done.12
  0.9 0.0 copy-done.14
  0.9 0.0 copy-done.15
  0.9 0.0 copy-done.16
  0.9 0.0 copy-start
  0.9 1.1 %copy-done = bf16[768,512]{1,0:T(8,128)(2,1)S(1)} copy-done((bf16[768,512]{1,0:T(8,128)(2,1)S(1)}, bf16[768,512]{1,0:T(8,128)(2,1)}, u32[]{:S(2)}) %copy-start) | copy-done | bytes 786456
  2.0 0.0 copy-start.1
  2.0 1.0 %copy-done.1 = f32[2,16,2816]{2,1,0:T(8,128)S(1)} copy-done((f32[2,16,2816]{2,1,0:T(8,128)S(1)}, f32[2,16,2816]{2,1,0:T(8,128)}, u32[]{:S(2)}) %copy-start.1) | copy-done | bytes 360472
  3.0 0.0 copy-start.2
  3.0 0.9 %copy-done.2 = bf16[2,256,256]{2,1,0:T(8,128)(2,1)S(1)} copy-done((bf16[2,256,256]{2,1,0:T(8,128)(2,1)S(1)}, bf16[2,256,256]{2,1,0:T(8,128)(2,1)}, u32[]{:S(2)}) %copy-start.2) | copy-done | bytes 262168
  4.0 0.0 copy-start.3
  4.0 0.9 %copy-done.3 = bf16[2,120,512]{2,1,0:T(8,128)(2,1)S(1)} copy-done((bf16[2,120,512]{2,1,0:T(8,128)(2,1)S(1)}, bf16[2,120,512]{2,1,0:T(8,128)(2,1)}, u32[]{:S(2)}) %copy-start.3) | copy-done | bytes 245784
  4.9 0.0 copy-start.4
  4.9 0.9 %copy-done.4 = bf16[384,256]{1,0:T(8,128)(2,1)S(1)} copy-done((bf16[384,256]{1,0:T(8,128)(2,1)S(1)}, bf16[384,256]{1,0:T(8,128)(2,1)}, u32[]{:S(2)}) %copy-start.4) | copy-done | bytes 196632
  5.8 0.0 copy-start.5
  5.8 0.9 %copy-done.5 = bf16[1,320,256]{2,1,0:T(8,128)(2,1)S(1)} copy-done((bf16[1,320,256]{2,1,0:T(8,128)(2,1)S(1)}, bf16[1,320,256]{2,1,0:T(8,128)(2,1)}, u32[]{:S(2)}) %copy-start.5) | copy-done | bytes 163864
  6.7 0.0 copy-start.6
  6.7 0.9 %copy-done.6 = f32[128,256]{1,0:T(8,128)S(1)} copy-done((f32[128,256]{1,0:T(8,128)S(1)}, f32[128,256]{1,0:T(8,128)}, u32[]{:S(2)}) %copy-start.6) | copy-done | bytes 131096
  7.6 0.0 copy-start.7
  7.6 0.9 %copy-done.7 = bf16[256,256]{1,0:T(8,128)(2,1)S(1)} copy-done((bf16[256,256]{1,0:T(8,128)(2,1)S(1)}, bf16[256,256]{1,0:T(8,128)(2,1)}, u32[]{:S(2)}) %copy-start.7) | copy-done | bytes 131096
  8.5 0.0 copy-start.8
  8.6 0.9 %copy-done.8 = bf16[256,256]{1,0:T(8,128)(2,1)S(1)} copy-done((bf16[256,256]{1,0:T(8,128)(2,1)S(1)}, bf16[256,256]{1,0:T(8,128)(2,1)}, u32[]{:S(2)}) %copy-start.8) | copy-done | bytes 131096
  9.5 0.0 copy-start.9
  9.5 0.9 %copy-done.9 = bf16[2,104,256]{2,1,0:T(8,128)(2,1)S(1)} copy-done((bf16[2,104,256]{2,1,0:T(8,128)(2,1)S(1)}, bf16[2,104,256]{2,1,0:T(8,128)(2,1)}, u32[]{:S(2)}) %copy-start.9) | copy-done | bytes 106520
  10.3 0.0 copy-start.10
  10.4 0.9 %copy-done.10 = bf16[2,104,256]{2,1,0:T(8,128)(2,1)S(1)} copy-done((bf16[2,104,256]{2,1,0:T(8,128)(2,1)S(1)}, bf16[2,104,256]{2,1,0:T(8,128)(2,1)}, u32[]{:S(2)}) %copy-start.10) | copy-done | bytes 106520
  11.2 0.0 copy-start.13
  11.2 0.7 %copy-done.13 = f32[2,8,1,128]{3,2,1,0:T(1,128)S(1)} copy-done((f32[2,8,1,128]{3,2,1,0:T(1,128)S(1)}, f32[2,8,1,128]{3,2,1,0:T(1,128)}, u32[]{:S(2)}) %copy-start.13) | copy-done | bytes 8216
  11.9 27.9 %shard_map.172 = f32[1,320,256]{2,1,0:T(8,128)S(1)} custom-call(s32[1,2]{1,0:T(1,128)S(1)} %copy-done.14, bf16[1,320,256]{2,1,0:T(8,128)(2,1)S(1)} %copy-done.5, bf16[256,256]{1,0:T(8,128)(2,1)S(1)} %copy-done.8, s32[1,2560]{1,0:T(1,128)S(1)} %copy-done.12, f32[2,16,2816]{2,1,0:T(8,128)S(1)} %copy-done.1, f32[1,128]{1,0:T(1,128)S(1)} %bitcast.2, ...), custom_call_target="tpu_custom_call" | custom-call | tf_op jit(solution)/shard_map/pallas_call | solution.py:489
  39.8 0.7 %copy.21 = f32[1,320,256]{2,1,0:T(8,128)} copy(f32[1,320,256]{2,1,0:T(8,128)S(1)} %shard_map.172) | data formatting | bytes 655360
Async XLA Ops:
  0.0 0.9 %copy-start.11 = (f32[2,8,1,256]{3,2,1,0:T(1,128)S(1)}, f32[2,8,1,256]{3,2,1,0:T(1,128)}, u32[]{:S(2)}) copy-start(f32[2,8,1,256]{3,2,1,0:T(1,128)} %constant.29.clone.refs_13_) | copy-start | bytes 49156
  0.0 0.9 %copy-start.12 = (s32[1,2560]{1,0:T(1,128)S(1)}, s32[1,2560]{1,0:T(1,128)}, u32[]{:S(2)}) copy-start(s32[1,2560]{1,0:T(1,128)} %refs_2_.1) | copy-start | bytes 30724
  0.0 0.9 %copy-start.14 = (s32[1,2]{1,0:T(1,128)S(1)}, s32[1,2]{1,0:T(1,128)}, u32[]{:S(2)}) copy-start(s32[1,2]{1,0:T(1,128)} %near_ref.1) | copy-start | bytes 28
  0.0 0.9 %copy-start.15 = (f32[128]{0:T(128)S(1)}, f32[128]{0:T(128)}, u32[]{:S(2)}) copy-start(f32[128]{0:T(128)} %param.22) | copy-start | bytes 1540
  0.0 0.9 %copy-start.16 = (f32[128]{0:T(128)S(1)}, f32[128]{0:T(128)}, u32[]{:S(2)}) copy-start(f32[128]{0:T(128)} %param.23) | copy-start | bytes 1540
  0.9 1.1 %copy-start = (bf16[768,512]{1,0:T(8,128)(2,1)S(1)}, bf16[768,512]{1,0:T(8,128)(2,1)}, u32[]{:S(2)}) copy-start(bf16[768,512]{1,0:T(8,128)(2,1)} %constant.24.clone.refs_8_) | copy-start | bytes 2359300
  2.0 1.0 %copy-start.1 = (f32[2,16,2816]{2,1,0:T(8,128)S(1)}, f32[2,16,2816]{2,1,0:T(8,128)}, u32[]{:S(2)}) copy-start(f32[2,16,2816]{2,1,0:T(8,128)} %refs_3_.1) | copy-start | bytes 1081348
  3.0 0.9 %copy-start.2 = (bf16[2,256,256]{2,1,0:T(8,128)(2,1)S(1)}, bf16[2,256,256]{2,1,0:T(8,128)(2,1)}, u32[]{:S(2)}) copy-start(bf16[2,256,256]{2,1,0:T(8,128)(2,1)} %constant.31.clone.refs_15_) | copy-start | bytes 786436
  4.0 0.9 %copy-start.3 = (bf16[2,120,512]{2,1,0:T(8,128)(2,1)S(1)}, bf16[2,120,512]{2,1,0:T(8,128)(2,1)}, u32[]{:S(2)}) copy-start(bf16[2,120,512]{2,1,0:T(8,128)(2,1)} %constant.27.clone.refs_11_) | copy-start | bytes 737284
  4.9 0.9 %copy-start.4 = (bf16[384,256]{1,0:T(8,128)(2,1)S(1)}, bf16[384,256]{1,0:T(8,128)(2,1)}, u32[]{:S(2)}) copy-start(bf16[384,256]{1,0:T(8,128)(2,1)} %constant.23.clone.refs_7_) | copy-start | bytes 589828
  5.8 0.9 %copy-start.5 = (bf16[1,320,256]{2,1,0:T(8,128)(2,1)S(1)}, bf16[1,320,256]{2,1,0:T(8,128)(2,1)}, u32[]{:S(2)}) copy-start(bf16[1,320,256]{2,1,0:T(8,128)(2,1)} %refs_0_.1) | copy-start | bytes 491524
  6.7 0.9 %copy-start.6 = (f32[128,256]{1,0:T(8,128)S(1)}, f32[128,256]{1,0:T(8,128)}, u32[]{:S(2)}) copy-start(f32[128,256]{1,0:T(8,128)} %constant.32.clone.refs_16_) | copy-start | bytes 393220
  7.6 0.9 %copy-start.7 = (bf16[256,256]{1,0:T(8,128)(2,1)S(1)}, bf16[256,256]{1,0:T(8,128)(2,1)}, u32[]{:S(2)}) copy-start(bf16[256,256]{1,0:T(8,128)(2,1)} %constant.30.clone.refs_14_) | copy-start | bytes 393220
  8.5 0.9 %copy-start.8 = (bf16[256,256]{1,0:T(8,128)(2,1)S(1)}, bf16[256,256]{1,0:T(8,128)(2,1)}, u32[]{:S(2)}) copy-start(bf16[256,256]{1,0:T(8,128)(2,1)} %constant.22.clone.refs_1_) | copy-start | bytes 393220
  9.5 0.9 %copy-start.9 = (bf16[2,104,256]{2,1,0:T(8,128)(2,1)S(1)}, bf16[2,104,256]{2,1,0:T(8,128)(2,1)}, u32[]{:S(2)}) copy-start(bf16[2,104,256]{2,1,0:T(8,128)(2,1)} %constant.26.clone.refs_10_) | copy-start | bytes 319492
  10.3 0.9 %copy-start.10 = (bf16[2,104,256]{2,1,0:T(8,128)(2,1)S(1)}, bf16[2,104,256]{2,1,0:T(8,128)(2,1)}, u32[]{:S(2)}) copy-start(bf16[2,104,256]{2,1,0:T(8,128)(2,1)} %constant.25.clone.refs_9_) | copy-start | bytes 319492
  11.2 0.7 %copy-start.13 = (f32[2,8,1,128]{3,2,1,0:T(1,128)S(1)}, f32[2,8,1,128]{3,2,1,0:T(1,128)}, u32[]{:S(2)}) copy-start(f32[2,8,1,128]{3,2,1,0:T(1,128)} %constant.28.clone.refs_12_) | copy-start | bytes 24580
where the time goes:
time: 41 us; the launch traced here: 40.5 us
  Pallas kernels  27.9 us (68%)
  local copies, waits for them, and re-layouts  12.6 us (31%)
    pallas_call x1, Pallas kernels, body(): pl.pallas_call(kernel, out_shape=jax.ShapeDtypeStruct(frames.shape, f32),...  27.9 us
    unnamed x36, local copies, waits for them, and re-layouts  12.6 us

commit v1 on v0

--- a/solution.py
+++ b/solution.py
@@ -269,7 +269,7 @@
     row_index = lax.broadcasted_iota(jnp.int32, (OUTS, SHARE // BC), 0) // (BC // RADIX)
     col_index = lax.broadcasted_iota(jnp.int32, (OUTS, SHARE // BC), 1)
     pick = jnp.where(row_index == col_index, 1.0, 0.0)
-    inside = mul(pick, inside)
+    inside = mul_nt(pick, inside)
     row_index = lax.broadcasted_iota(jnp.int32, (TICKS // BT, TICKS), 0)
     col_index = lax.broadcasted_iota(jnp.int32, (TICKS // BT, TICKS), 1) // BT
     inside = mul(inside, jnp.where(row_index == col_index, 1.0, 0.0))
@@ -444,7 +444,7 @@
         kern,
         wide.reshape(1, FREQS),
         tight.reshape(1, FREQS),
-        roi,
+        jnp.swapaxes(roi, 1, 2),
         jnp.asarray(forward_dense(NU, 128)),
         jnp.asarray(forward_dense(NW, 256)),
         jnp.asarray(inverse_dense(NU, 128, PU, 0, NU, 0, 104)),
@@ -489,11 +489,11 @@
     return pl.pallas_call(
         kernel,
         out_shape=jax.ShapeDtypeStruct(frames.shape, f32),
-        in_specs=[pl.BlockSpec(memory_space=pltpu.SMEM)] + [pl.BlockSpec(memory_space=pl.ANY)] * len(arrays),
-        out_specs=pl.BlockSpec(memory_space=pl.ANY),
+        in_specs=[pl.BlockSpec(memory_space=pltpu.SMEM)] + [pl.BlockSpec(memory_space=pltpu.HBM)] * len(arrays),
+        out_specs=pl.BlockSpec(memory_space=pltpu.HBM),
         scratch_shapes=scratch,
         compiler_params=pltpu.CompilerParams(
-            collective_id=0, has_side_effects=True, vmem_limit_bytes=48 * 1024 * 1024
+            collective_id=0, has_side_effects=True, vmem_limit_bytes=60 * 1024 * 1024
         ),
     )(near, *arrays)
 

time: 41 us -> 28.6 us (0.70)
  local copies, waits for them, and re-layouts: 12.6 us -> 1.72 us
  Pallas kernels: 27.9 us -> 26.8 us
    unnamed x36 -> x1, local copies, waits for them, and re-layouts: 12.6 us -> 1.72 us
    pallas_call x1, Pallas kernels: 27.9 us -> 26.8 us  [body(): pl.pallas_call(kernel, out_shape=jax.ShapeDtypeStruct(frames.shape, f32),...]
where the time goes in v1:
time: 28.6 us; the launch traced here: 28.5 us
  Pallas kernels  26.8 us (94%)
  local copies, waits for them, and re-layouts  1.72 us (6%)
    pallas_call x1, Pallas kernels, body(): pl.pallas_call(kernel, out_shape=jax.ShapeDtypeStruct(frames.shape, f32),...  26.8 us
    unnamed x1, local copies, waits for them, and re-layouts  1.72 us

profile of v1, /device:TPU:10, one launch (start us, length us, event | category | flops | bytes accessed | tf_op | source)
XLA Modules:
  0.0 28.5 jit_solution(9248701255478787595)
XLA Ops:
  0.0 26.8 %shard_map.172 = f32[1,320,256]{2,1,0:T(8,128)} custom-call(s32[1,2]{1,0:T(1,128)} %near_ref.1, bf16[1,320,256]{2,1,0:T(8,128)(2,1)} %refs_0_.1, bf16[256,256]{1,0:T(8,128)(2,1)} %constant.22.clone.refs_1_, s32[1,2560]{1,0:T(1,128)} %refs_2_.1, f32[2,16,2816]{2,1,0:T(8,128)} %refs_3_.1, f32[1,128]{1,0:T(1,128)} %bitcast.4, f32[1,128]{1,0:T(1,128)} %bitcast.5, ...), custom_call_target="tpu_custom_call" | custom-call | tf_op jit(solution)/shard_map/pallas_call | solution.py:489
  26.8 1.7 %copy.20 = f32[1,320,256]{2,1,0:T(8,128)} copy(f32[1,320,256]{2,1,0:T(8,128)} %shard_map.172) | data formatting | bytes 655360

commit v2 on v1

--- a/solution.py
+++ b/solution.py
@@ -100,12 +100,16 @@
     return (np.arange(256)[:, None] == place[None, :]).astype(np.float32).astype(bf16)
 
 
-def mask_rows():
-    return (np.arange(OUTS)[:, None] // (BC // RADIX) == np.arange(SHARE // BC)[None, :]).astype(np.float32)
-
-
-def mask_columns():
-    return (np.arange(TICKS // BT)[:, None] == np.arange(TICKS)[None, :] // BT).astype(np.float32)
+def levels_of(largest):
+    return jnp.ceil(jnp.log2(jnp.maximum(largest, 1e-30)) * STEPS)
+
+
+def to_short(value):
+    return value.astype(jnp.int32).astype(jnp.int16)
+
+
+def from_short(value):
+    return value.astype(jnp.int32).astype(f32)
 
 
 def split(value):
@@ -178,6 +182,12 @@
     return mul_nt(table[0], high) + mul_nt(table[1], high) + mul_nt(table[0], low)
 
 
+def message(part):
+    level = levels_of(jnp.max(jnp.abs(part), axis=0, keepdims=True))
+    scaled = jnp.round(part * (LEVELS * jnp.exp2(-level / STEPS)))
+    return to_short(jnp.concatenate([scaled, jnp.broadcast_to(level, (8, 256))], axis=0))
+
+
 def kernel_window(kern, part, start, length, width):
     base = start // 128 * 128
     span = -(-(start - base + length) // 128) * 128
@@ -188,10 +198,12 @@
     return piece[:, :width]
 
 
-INPUTS = 17
-
-
-def body_kernel(apas, near, *refs):
+INPUTS = 18
+LEVELS = 32000.0
+STEPS = 8.0
+
+
+def body_kernel(apas, *refs):
     hbm = refs[:INPUTS]
     out = refs[INPUTS]
     local = refs[INPUTS + 1 : 2 * INPUTS + 1]
@@ -199,29 +211,39 @@
         2 * INPUTS + 1 : 2 * INPUTS + 16
     ]
     in_sem, send1, recv1, send2, recv2, sendh, recvh, out_sem = refs[2 * INPUTS + 16 :]
-    (frames, ticks, links, kern, wide, tight, roi, fwd_u, fwd_w, inv_u, inv_v, inv_w, tw_u, tw_w, rim, back, expand) = local
+    (frames, ticks, links, kern, wide, tight, roi, fwd_u, fwd_w, inv_u, inv_v, inv_w, tw_u, tw_w, rim, back, expand, near) = local
 
     me = lax.axis_index("chan")
     apa = lax.axis_index("apa")
     after = lax.rem(apa + 1, apas)
     before = lax.rem(apa + apas - 1, apas)
 
+    barrier = pltpu.get_barrier_semaphore()
+    for step in range(1, CHAN):
+        pl.semaphore_signal(barrier, inc=1, device_id={"chan": lax.rem(me + step, CHAN)}, device_id_type=MESH)
+    @pl.when(apa < apas - 1)
+    def _():
+        pl.semaphore_signal(barrier, inc=1, device_id={"apa": after}, device_id_type=MESH)
+    @pl.when(apa > 0)
+    def _():
+        pl.semaphore_signal(barrier, inc=1, device_id={"apa": before}, device_id_type=MESH)
+
     loads = [pltpu.make_async_copy(hbm[i], local[i], in_sem.at[i]) for i in range(INPUTS)]
     for load in loads:
         load.start()
 
-    barrier = pltpu.get_barrier_semaphore()
-    for step in range(1, CHAN):
-        pl.semaphore_signal(barrier, inc=1, device_id={"chan": lax.rem(me + step, CHAN)}, device_id_type=MESH)
-    pl.semaphore_signal(barrier, inc=1, device_id={"apa": after}, device_id_type=MESH)
-    pl.semaphore_signal(barrier, inc=1, device_id={"apa": before}, device_id_type=MESH)
-
     loads[0].wait()
     loads[1].wait()
     padded = jnp.concatenate([frames[0], jnp.zeros((PAD - SHARE, TICKS), bf16)], axis=0)
-    tx1[...] = mul_nt(ticks[...], padded).reshape(CHAN, ROWS, PAD)
-
-    pl.semaphore_wait(barrier, CHAN + 1)
+    spectra = mul_nt(ticks[...], padded)
+    level = levels_of(jnp.max(jnp.abs(spectra), axis=1, keepdims=True))
+    scaled = jnp.round(spectra * (LEVELS * jnp.exp2(-level / STEPS)))
+    lane = lax.broadcasted_iota(jnp.int32, scaled.shape, 1)
+    tx1[...] = to_short(jnp.where(lane < SHARE, scaled, level)).reshape(CHAN, ROWS, PAD)
+
+    first = apa == 0
+    final = apa == apas - 1
+    pl.semaphore_wait(barrier, CHAN + 1 - first.astype(jnp.int32) - final.astype(jnp.int32))
 
     def first_copy(step):
         dest = lax.rem(me + step, CHAN)
@@ -286,24 +308,29 @@
         ).wait_recv()
     for s in range(CHAN):
         lanes = slice(s * PAD, (s + 1) * PAD)
-        high, low = split(rx1[s])
+        value = from_short(rx1[s])
+        high, low = split(value * (jnp.exp2(value[:, SHARE : SHARE + 1] / STEPS) / LEVELS))
         small[0:ROWS, lanes] = high
         small[ROWS : 2 * ROWS, lanes] = low
-        for h in range(RADIX):
-            mask = jnp.concatenate([masks[s, h], masks[s, h]], axis=0)
-            big[h * ROWS : (h + 1) * ROWS, lanes] = high * mask
-            big[256 + h * ROWS : 256 + (h + 1) * ROWS, lanes] = low * mask
 
     bands = mul_nt(small[...], edge[...])
     first_band = bands[:, :HALO]
     last_band = bands[:, HALO:]
-    lower = near[0, 0]
-    upper = near[0, 1]
+    lower = jnp.broadcast_to(near[:, 0:1], first_band.shape)
+    upper = jnp.broadcast_to(near[:, 1:2], first_band.shape)
     none = jnp.zeros_like(first_band)
     to_after = jnp.where(upper == after, last_band, jnp.where(lower == after, first_band, none))
     to_before = jnp.where(lower == before, first_band, jnp.where(upper == before, last_band, none))
     txh[0] = to_after.astype(bf16)
     txh[1] = to_before.astype(bf16)
+
+    @pl.when(apa == 0)
+    def _():
+        rxh[0] = jnp.zeros((2 * ROWS, HALO), bf16)
+
+    @pl.when(apa == apas - 1)
+    def _():
+        rxh[1] = jnp.zeros((2 * ROWS, HALO), bf16)
 
     def edge_copy(way):
         return pltpu.make_async_remote_copy(
@@ -315,9 +342,20 @@
             device_id_type=MESH,
         )
 
-    edge_copy(0).start()
-    edge_copy(1).start()
-
+    @pl.when(apa < apas - 1)
+    def _():
+        edge_copy(0).start()
+
+    @pl.when(apa > 0)
+    def _():
+        edge_copy(1).start()
+
+    for s in range(CHAN):
+        lanes = slice(s * PAD, (s + 1) * PAD)
+        for h in range(RADIX):
+            mask = jnp.concatenate([masks[s, h], masks[s, h]], axis=0)
+            big[h * ROWS : (h + 1) * ROWS, lanes] = small[0:ROWS, lanes] * mask
+            big[256 + h * ROWS : 256 + (h + 1) * ROWS, lanes] = small[ROWS : 2 * ROWS, lanes] * mask
     placed = mul_nt(big[...], onehot[...])
 
     def second_copy(dest):
@@ -349,17 +387,18 @@
 
     part_u = plane(slice(0, 128), fwd_u, kern_u, tw_u, inv_u, 128)
     part_v = plane(slice(128, 256), fwd_u, kern_v, tw_u, inv_v, 128)
-    tx2[0] = part_u[0:40]
-    tx2[1] = part_u[40:80]
-    tx2[2, 0:16] = part_u[80:96]
-    tx2[2, 16:24] = part_u[96:104] + part_v[0:8]
-    tx2[2, 24:40] = part_v[8:24]
-    tx2[3] = part_v[24:64]
-    tx2[4] = part_v[64:104]
+    middle = jnp.concatenate([part_u[80:96], part_u[96:104] + part_v[0:8], part_v[8:24]], axis=0)
+    for dest, part in enumerate([part_u[0:40], part_u[40:80], middle, part_v[24:64], part_v[64:104]]):
+        tx2[dest] = message(part)
     send_on(range(0, 5))
 
-    edge_copy(0).wait_recv()
-    edge_copy(1).wait_recv()
+    @pl.when(apa > 0)
+    def _():
+        edge_copy(0).wait_recv()
+
+    @pl.when(apa < apas - 1)
+    def _():
+        edge_copy(1).wait_recv()
     from_before = rxh[0].astype(f32)
     from_after = rxh[1].astype(f32)
     blank = jnp.zeros_like(from_before)
@@ -376,9 +415,8 @@
     low = full[256:512].astype(bf16)
     product = mul(jnp.concatenate([high, low, high], axis=1), fwd_w[...])
     part_w = inverse_product(inv_w, channel_product(product, kern_w, tw_w, 256))
-    tx2[5] = part_w[0:40]
-    tx2[6] = part_w[40:80]
-    tx2[7] = part_w[80:120]
+    for dest in range(3):
+        tx2[5 + dest] = message(part_w[dest * OUTS : (dest + 1) * OUTS])
     send_on(range(5, 8))
 
     for step in range(1, CHAN):
@@ -394,11 +432,15 @@
 
     block = lax.broadcasted_iota(jnp.int32, (OUTS, 128), 1) // ROWS
     columns = []
+    pieces = []
+    for s in range(CHAN):
+        value = from_short(rx2[s])
+        pieces.append(value[:OUTS] * (jnp.exp2(value[OUTS : OUTS + 1] / STEPS) / LEVELS))
     for side in range(2):
         for c in range(RADIX):
             acc = None
             for q in range(4):
-                piece = rx2[4 * side + q, :, c // 4 * 128 : (c // 4 + 1) * 128]
+                piece = pieces[4 * side + q][:, c // 4 * 128 : (c // 4 + 1) * 128]
                 turn = (q - c % 4) % 4 * ROWS
                 if turn:
                     piece = pltpu.roll(piece, turn, axis=1)
@@ -431,8 +473,13 @@
     for step in range(1, CHAN):
         first_copy(step).wait_send()
         second_copy(lax.rem(me + step, CHAN)).wait_send()
-    edge_copy(0).wait_send()
-    edge_copy(1).wait_send()
+    @pl.when(apa < apas - 1)
+    def _():
+        edge_copy(0).wait_send()
+
+    @pl.when(apa > 0)
+    def _():
+        edge_copy(1).wait_send()
 
 
 def body(frames, links, near, kern, wide, tight, roi):
@@ -455,13 +502,14 @@
         jnp.asarray(rim_places()),
         jnp.asarray(inverse_ticks()),
         jnp.asarray(spread_filters()),
+        near,
     ]
     scratch = [pltpu.VMEM(a.shape, a.dtype) for a in arrays]
     scratch += [
-        pltpu.VMEM((CHAN, ROWS, PAD), f32),
-        pltpu.VMEM((CHAN, ROWS, PAD), f32),
-        pltpu.VMEM((CHAN, OUTS, 256), f32),
-        pltpu.VMEM((CHAN, OUTS, 256), f32),
+        pltpu.VMEM((CHAN, ROWS, PAD), jnp.int16),
+        pltpu.VMEM((CHAN, ROWS, PAD), jnp.int16),
+        pltpu.VMEM((CHAN, OUTS + 8, 256), jnp.int16),
+        pltpu.VMEM((CHAN, OUTS + 8, 256), jnp.int16),
         pltpu.VMEM((2, 2 * ROWS, HALO), bf16),
         pltpu.VMEM((2, 2 * ROWS, HALO), bf16),
         pltpu.VMEM((512, LINKS), bf16),
@@ -483,19 +531,20 @@
         pltpu.SemaphoreType.DMA((2,)),
     ]
 
-    def kernel(near_ref, *refs):
-        body_kernel(apas, near_ref, *refs)
-
-    return pl.pallas_call(
+    def kernel(*refs):
+        body_kernel(apas, *refs)
+
+    halves_out = pl.pallas_call(
         kernel,
         out_shape=jax.ShapeDtypeStruct(frames.shape, f32),
-        in_specs=[pl.BlockSpec(memory_space=pltpu.SMEM)] + [pl.BlockSpec(memory_space=pltpu.HBM)] * len(arrays),
-        out_specs=pl.BlockSpec(memory_space=pltpu.HBM),
+        in_specs=[pl.BlockSpec(memory_space=pltpu.HBM)] * len(arrays),
+        out_specs=pl.BlockSpec(memory_space=pl.ANY),
         scratch_shapes=scratch,
         compiler_params=pltpu.CompilerParams(
-            collective_id=0, has_side_effects=True, vmem_limit_bytes=60 * 1024 * 1024
+            collective_id=0, has_side_effects=True, vmem_limit_bytes=40 * 1024 * 1024
         ),
-    )(near, *arrays)
+    )(*[pltpu.with_memory_space_constraint(a, pltpu.HBM) for a in arrays])
+    return halves_out
 
 
 def solution(mesh):

time: 28.6 us -> 23 us (0.80)
  the two profiles are of different devices: /device:TPU:10 before, /device:TPU:14 now
where the time goes in v2:
time: 23 us; the launch traced here: 22.9 us
  Pallas kernels  22.2 us (97%)
  local copies, waits for them, and re-layouts  0.73 us (3%)
    pallas_call x1, Pallas kernels, body(): pl.pallas_call(kernel, out_shape=jax.ShapeDtypeStruct(frames.shape, f32),...  22.2 us
    unnamed x1, local copies, waits for them, and re-layouts  0.73 us

profile of v2, /device:TPU:14, one launch (start us, length us, event | category | flops | bytes accessed | tf_op | source)
XLA Modules:
  0.0 22.9 jit_solution(12161335349331796031)
XLA Ops:
  0.0 22.2 %shard_map.172 = f32[1,320,256]{2,1,0:T(8,128)S(1)} custom-call(bf16[1,320,256]{2,1,0:T(8,128)(2,1)} %refs_0_.1, bf16[256,256]{1,0:T(8,128)(2,1)} %constant.22.clone.refs_1_, s32[1,2560]{1,0:T(1,128)} %refs_2_.1, f32[2,16,2816]{2,1,0:T(8,128)} %refs_3_.1, f32[1,128]{1,0:T(1,128)} %bitcast.4, f32[1,128]{1,0:T(1,128)} %bitcast.5, s32[1,4,20]{2,1,0:T(4,128)} %bitcast.3, ...), custom_call_target="tpu_custom_call" | custom-call | tf_op jit(solution)/shard_map/pallas_call | solution.py:537
  22.2 0.7 %copy.20 = f32[1,320,256]{2,1,0:T(8,128)} copy(f32[1,320,256]{2,1,0:T(8,128)S(1)} %shard_map.172) | data formatting | bytes 655360

commit v3 on v2

--- a/solution.py
+++ b/solution.py
@@ -27,7 +27,6 @@
 NU = PU // RADIX
 PE = PW + 2 * HALO
 NW = PE // RADIX
-LINKS = CHAN * PAD
 OUTS = SHARE // RADIX
 
 MESH = pl.DeviceIdType.MESH
@@ -185,7 +184,7 @@
 def message(part):
     level = levels_of(jnp.max(jnp.abs(part), axis=0, keepdims=True))
     scaled = jnp.round(part * (LEVELS * jnp.exp2(-level / STEPS)))
-    return to_short(jnp.concatenate([scaled, jnp.broadcast_to(level, (8, 256))], axis=0))
+    return to_short(jnp.concatenate([scaled, jnp.broadcast_to(level, (8, part.shape[1]))], axis=0))
 
 
 def kernel_window(kern, part, start, length, width):
@@ -207,27 +206,27 @@
     hbm = refs[:INPUTS]
     out = refs[INPUTS]
     local = refs[INPUTS + 1 : 2 * INPUTS + 1]
-    (tx1, rx1, tx2, rx2, txh, rxh, onehot, edge, masks, big, small, kern_u, kern_v, kern_w, result) = refs[
-        2 * INPUTS + 1 : 2 * INPUTS + 16
+    (tx1, rx1, tx2, rx2, txh, rxh, onehot, masks, big, kern_u, kern_v, kern_w, result) = refs[
+        2 * INPUTS + 1 : 2 * INPUTS + 14
     ]
-    in_sem, send1, recv1, send2, recv2, sendh, recvh, out_sem = refs[2 * INPUTS + 16 :]
+    in_sem, send1, recv1, send2, recv2, sendh, recvh, entered, out_sem = refs[2 * INPUTS + 14 :]
     (frames, ticks, links, kern, wide, tight, roi, fwd_u, fwd_w, inv_u, inv_v, inv_w, tw_u, tw_w, rim, back, expand, near) = local
 
     me = lax.axis_index("chan")
     apa = lax.axis_index("apa")
-    after = lax.rem(apa + 1, apas)
-    before = lax.rem(apa + apas - 1, apas)
+    after = apa + 1
+    before = apa - 1
+    has_after = apa < apas - 1
+    has_before = apa > 0
+    even = lax.rem(apa, 2) == 0
+    wait_after = has_after & (even | (after == apas // 2))
+    wait_before = has_before & even & (apa != apas // 2)
+    greet_after = has_after & jnp.logical_not(wait_after)
+    greet_before = has_before & jnp.logical_not(wait_before)
 
     barrier = pltpu.get_barrier_semaphore()
     for step in range(1, CHAN):
         pl.semaphore_signal(barrier, inc=1, device_id={"chan": lax.rem(me + step, CHAN)}, device_id_type=MESH)
-    @pl.when(apa < apas - 1)
-    def _():
-        pl.semaphore_signal(barrier, inc=1, device_id={"apa": after}, device_id_type=MESH)
-    @pl.when(apa > 0)
-    def _():
-        pl.semaphore_signal(barrier, inc=1, device_id={"apa": before}, device_id_type=MESH)
-
     loads = [pltpu.make_async_copy(hbm[i], local[i], in_sem.at[i]) for i in range(INPUTS)]
     for load in loads:
         load.start()
@@ -241,9 +240,15 @@
     lane = lax.broadcasted_iota(jnp.int32, scaled.shape, 1)
     tx1[...] = to_short(jnp.where(lane < SHARE, scaled, level)).reshape(CHAN, ROWS, PAD)
 
-    first = apa == 0
-    final = apa == apas - 1
-    pl.semaphore_wait(barrier, CHAN + 1 - first.astype(jnp.int32) - final.astype(jnp.int32))
+    pl.semaphore_wait(barrier, CHAN - 1 + wait_after.astype(jnp.int32) + wait_before.astype(jnp.int32))
+
+    @pl.when(greet_after)
+    def _():
+        pl.semaphore_signal(barrier, inc=1, device_id={"apa": after}, device_id_type=MESH)
+
+    @pl.when(greet_before)
+    def _():
+        pl.semaphore_signal(barrier, inc=1, device_id={"apa": before}, device_id_type=MESH)
 
     def first_copy(step):
         dest = lax.rem(me + step, CHAN)
@@ -260,21 +265,76 @@
         first_copy(step).start()
     rx1[me] = tx1[me]
 
+    @pl.when(wait_after)
+    def _():
+        pl.semaphore_signal(entered.at[1], inc=1, device_id={"apa": after}, device_id_type=MESH)
+
+    @pl.when(wait_before)
+    def _():
+        pl.semaphore_signal(entered.at[0], inc=1, device_id={"apa": before}, device_id_type=MESH)
+
     loads[2].wait()
+    loads[17].wait()
+    mine = jnp.zeros((1, SHARE), jnp.int32)
     for s in range(CHAN):
-        wire = links[:, s * SHARE : (s + 1) * SHARE]
-        wire = jnp.concatenate([wire, jnp.full((1, PAD - SHARE), -8, jnp.int32)], axis=1)
+        mine = jnp.where(me == s, links[:, s * SHARE : (s + 1) * SHARE], mine)
+    mine = jnp.concatenate([mine, jnp.full((1, PAD - SHARE), -8, jnp.int32)], axis=1)
+    row = lax.broadcasted_iota(jnp.int32, (2 * HALO, PAD), 0)
+    spot = row + jnp.where(row >= HALO, CHANNELS - 2 * HALO, PU + PV)
+    local_edge = jnp.where(spot == mine, 1.0, 0.0).astype(bf16)
+    high, low = split(spectra)
+    bands = mul_nt(high, local_edge) + mul_nt(low, local_edge)
+    first_band = bands[:, :HALO]
+    last_band = bands[:, HALO:]
+    lower = jnp.broadcast_to(near[:, 0:1], first_band.shape)
+    upper = jnp.broadcast_to(near[:, 1:2], first_band.shape)
+    none = jnp.zeros_like(first_band)
+    to_after = jnp.where(upper == after, last_band, jnp.where(lower == after, first_band, none))
+    to_before = jnp.where(lower == before, first_band, jnp.where(upper == before, last_band, none))
+    for way, band in enumerate([to_after, to_before]):
+        for dest in range(CHAN):
+            txh[way, dest] = message(band[dest * ROWS : (dest + 1) * ROWS])
+
+    def edge_copy(way, dest):
+        return pltpu.make_async_remote_copy(
+            src_ref=txh.at[way, dest],
+            dst_ref=rxh.at[way, me],
+            send_sem=sendh.at[way, dest],
+            recv_sem=recvh.at[way, me],
+            device_id={"apa": after if way == 0 else before, "chan": dest},
+            device_id_type=MESH,
+        )
+
+    def send_edges(way):
+        for step in range(CHAN):
+            edge_copy(way, lax.rem(me + step, CHAN)).start()
+
+    @pl.when(wait_after)
+    def _():
+        send_edges(0)
+
+    @pl.when(wait_before)
+    def _():
+        send_edges(1)
+
+    @pl.when(apa == 0)
+    def _():
+        rxh[0] = jnp.zeros((CHAN, ROWS + 8, HALO), jnp.int16)
+
+    @pl.when(apa == apas - 1)
+    def _():
+        rxh[1] = jnp.zeros((CHAN, ROWS + 8, HALO), jnp.int16)
+
+    for part in range(5):
+        lanes = slice(part * 512, (part + 1) * 512)
+        wire = links[:, lanes]
         group = lax.shift_right_arithmetic(wire, 3)
         rest = lax.bitwise_and(wire, 7)
         place = group + jnp.where(wire >= PU + PV, 72, jnp.where(wire >= PU, 28, 0))
-        row = lax.broadcasted_iota(jnp.int32, (512, PAD), 0)
-        onehot[:, s * PAD : (s + 1) * PAD] = jnp.where(row == place, 1.0, 0.0).astype(bf16)
-        row = lax.broadcasted_iota(jnp.int32, (256, PAD), 0)
-        spot = row + jnp.where(row >= HALO, CHANNELS - 2 * HALO, PU + PV)
-        edge[:, s * PAD : (s + 1) * PAD] = jnp.where(spot == wire, 1.0, 0.0).astype(bf16)
+        row = lax.broadcasted_iota(jnp.int32, (512, 512), 0)
+        onehot[:, lanes] = jnp.where(row == place, 1.0, 0.0).astype(bf16)
         for h in range(RADIX):
-            here = jnp.where((rest == h) & (wire >= 0), 1.0, 0.0)
-            masks[s, h] = jnp.broadcast_to(here, (16, PAD)).astype(bf16)
+            masks[h, :, lanes] = jnp.broadcast_to(jnp.where(rest == h, 1.0, 0.0), (16, 512)).astype(bf16)
 
     loads[3].wait()
     for m in range(RADIX):
@@ -283,7 +343,7 @@
             kern_v[m, part] = kernel_window(kern, part, PU + NU * m, NU, 128)
             kern_w[m, part] = kernel_window(kern, part, PU + PV + NW * m, NW, 256)
 
-    for load in loads[4:]:
+    for load in loads[4:17]:
         load.wait()
     gains = jnp.concatenate([wide[...], tight[...], jnp.zeros((6, FREQS), f32)], axis=0)
     gains = jnp.dot(gains, expand[0:FREQS], precision=lax.Precision.HIGHEST, preferred_element_type=f32)
@@ -296,6 +356,16 @@
     col_index = lax.broadcasted_iota(jnp.int32, (TICKS // BT, TICKS), 1) // BT
     inside = mul(inside, jnp.where(row_index == col_index, 1.0, 0.0))
 
+    @pl.when(greet_after)
+    def _():
+        pl.semaphore_wait(entered.at[0], 1)
+        send_edges(0)
+
+    @pl.when(greet_before)
+    def _():
+        pl.semaphore_wait(entered.at[1], 1)
+        send_edges(1)
+
     for step in range(1, CHAN):
         source = lax.rem(me + step, CHAN)
         pltpu.make_async_remote_copy(
@@ -306,56 +376,17 @@
             device_id={"chan": source},
             device_id_type=MESH,
         ).wait_recv()
-    for s in range(CHAN):
-        lanes = slice(s * PAD, (s + 1) * PAD)
-        value = from_short(rx1[s])
-        high, low = split(value * (jnp.exp2(value[:, SHARE : SHARE + 1] / STEPS) / LEVELS))
-        small[0:ROWS, lanes] = high
-        small[ROWS : 2 * ROWS, lanes] = low
-
-    bands = mul_nt(small[...], edge[...])
-    first_band = bands[:, :HALO]
-    last_band = bands[:, HALO:]
-    lower = jnp.broadcast_to(near[:, 0:1], first_band.shape)
-    upper = jnp.broadcast_to(near[:, 1:2], first_band.shape)
-    none = jnp.zeros_like(first_band)
-    to_after = jnp.where(upper == after, last_band, jnp.where(lower == after, first_band, none))
-    to_before = jnp.where(lower == before, first_band, jnp.where(upper == before, last_band, none))
-    txh[0] = to_after.astype(bf16)
-    txh[1] = to_before.astype(bf16)
-
-    @pl.when(apa == 0)
-    def _():
-        rxh[0] = jnp.zeros((2 * ROWS, HALO), bf16)
-
-    @pl.when(apa == apas - 1)
-    def _():
-        rxh[1] = jnp.zeros((2 * ROWS, HALO), bf16)
-
-    def edge_copy(way):
-        return pltpu.make_async_remote_copy(
-            src_ref=txh.at[way],
-            dst_ref=rxh.at[way],
-            send_sem=sendh.at[way],
-            recv_sem=recvh.at[way],
-            device_id={"apa": after if way == 0 else before},
-            device_id_type=MESH,
-        )
-
-    @pl.when(apa < apas - 1)
-    def _():
-        edge_copy(0).start()
-
-    @pl.when(apa > 0)
-    def _():
-        edge_copy(1).start()
-
-    for s in range(CHAN):
-        lanes = slice(s * PAD, (s + 1) * PAD)
+    for pair in range(CHAN // 2):
+        lanes = slice(pair * 2 * SHARE, (pair + 1) * 2 * SHARE)
+        values = []
+        for s in (2 * pair, 2 * pair + 1):
+            value = from_short(rx1[s])
+            values.append(value[:, :SHARE] * (jnp.exp2(value[:, SHARE : SHARE + 1] / STEPS) / LEVELS))
+        high, low = split(jnp.concatenate(values, axis=1))
         for h in range(RADIX):
-            mask = jnp.concatenate([masks[s, h], masks[s, h]], axis=0)
-            big[h * ROWS : (h + 1) * ROWS, lanes] = small[0:ROWS, lanes] * mask
-            big[256 + h * ROWS : 256 + (h + 1) * ROWS, lanes] = small[ROWS : 2 * ROWS, lanes] * mask
+            mask = jnp.concatenate([masks[h, :, lanes], masks[h, :, lanes]], axis=0)
+            big[h * ROWS : (h + 1) * ROWS, lanes] = high * mask
+            big[256 + h * ROWS : 256 + (h + 1) * ROWS, lanes] = low * mask
     placed = mul_nt(big[...], onehot[...])
 
     def second_copy(dest):
@@ -392,23 +423,41 @@
         tx2[dest] = message(part)
     send_on(range(0, 5))
 
-    @pl.when(apa > 0)
-    def _():
-        edge_copy(0).wait_recv()
-
-    @pl.when(apa < apas - 1)
-    def _():
-        edge_copy(1).wait_recv()
-    from_before = rxh[0].astype(f32)
-    from_after = rxh[1].astype(f32)
+    def edge_arrivals(way):
+        for source in range(CHAN):
+            pltpu.make_async_remote_copy(
+                src_ref=txh.at[way, source],
+                dst_ref=rxh.at[way, source],
+                send_sem=sendh.at[way, source],
+                recv_sem=recvh.at[way, source],
+                device_id={"apa": before if way == 0 else after, "chan": source},
+                device_id_type=MESH,
+            ).wait_recv()
+
+    @pl.when(has_before)
+    def _():
+        edge_arrivals(0)
+
+    @pl.when(has_after)
+    def _():
+        edge_arrivals(1)
+
+    sums = []
+    for way in range(2):
+        total = jnp.zeros((ROWS, HALO), f32)
+        for source in range(CHAN):
+            value = from_short(rxh[way, source])
+            total = total + value[:ROWS] * (jnp.exp2(value[ROWS : ROWS + 1] / STEPS) / LEVELS)
+        sums.append(total)
+    from_before, from_after = sums
+    lower = lower[:ROWS]
+    upper = upper[:ROWS]
     blank = jnp.zeros_like(from_before)
     rim_low = jnp.where(lower == before, from_before, jnp.where(lower == after, from_after, blank))
     rim_up = jnp.where(upper == after, from_after, jnp.where(upper == before, from_before, blank))
     rims = jnp.concatenate([rim_low, rim_up], axis=1)
     lane = lax.bitwise_and(lax.broadcasted_iota(jnp.int32, (ROWS, 2 * HALO), 1), RADIX - 1)
-    spread = [
-        jnp.where(lane == h, rims[part * ROWS : (part + 1) * ROWS], 0.0) for part in range(2) for h in range(RADIX)
-    ]
+    spread = [jnp.where(lane == h, part.astype(f32), 0.0) for part in split(rims) for h in range(RADIX)]
     rim_part = mul_nt(jnp.concatenate(spread, axis=0).astype(bf16), rim[...])
     full = placed[:, 256:512] + rim_part
     high = full[0:256].astype(bf16)
@@ -473,13 +522,15 @@
     for step in range(1, CHAN):
         first_copy(step).wait_send()
         second_copy(lax.rem(me + step, CHAN)).wait_send()
-    @pl.when(apa < apas - 1)
-    def _():
-        edge_copy(0).wait_send()
-
-    @pl.when(apa > 0)
-    def _():
-        edge_copy(1).wait_send()
+    @pl.when(has_after)
+    def _():
+        for dest in range(CHAN):
+            edge_copy(0, dest).wait_send()
+
+    @pl.when(has_before)
+    def _():
+        for dest in range(CHAN):
+            edge_copy(1, dest).wait_send()
 
 
 def body(frames, links, near, kern, wide, tight, roi):
@@ -510,13 +561,11 @@
         pltpu.VMEM((CHAN, ROWS, PAD), jnp.int16),
         pltpu.VMEM((CHAN, OUTS + 8, 256), jnp.int16),
         pltpu.VMEM((CHAN, OUTS + 8, 256), jnp.int16),
-        pltpu.VMEM((2, 2 * ROWS, HALO), bf16),
-        pltpu.VMEM((2, 2 * ROWS, HALO), bf16),
-        pltpu.VMEM((512, LINKS), bf16),
-        pltpu.VMEM((256, LINKS), bf16),
-        pltpu.VMEM((CHAN, RADIX, 16, PAD), bf16),
-        pltpu.VMEM((512, LINKS), bf16),
-        pltpu.VMEM((2 * ROWS, LINKS), bf16),
+        pltpu.VMEM((2, CHAN, ROWS + 8, HALO), jnp.int16),
+        pltpu.VMEM((2, CHAN, ROWS + 8, HALO), jnp.int16),
+        pltpu.VMEM((512, CHANNELS), bf16),
+        pltpu.VMEM((RADIX, 16, CHANNELS), bf16),
+        pltpu.VMEM((512, CHANNELS), bf16),
         pltpu.VMEM((RADIX, 2, KB, 128), f32),
         pltpu.VMEM((RADIX, 2, KB, 128), f32),
         pltpu.VMEM((RADIX, 2, KB, 256), f32),
@@ -526,8 +575,9 @@
         pltpu.SemaphoreType.DMA((CHAN,)),
         pltpu.SemaphoreType.DMA((CHAN,)),
         pltpu.SemaphoreType.DMA((CHAN,)),
-        pltpu.SemaphoreType.DMA((2,)),
-        pltpu.SemaphoreType.DMA((2,)),
+        pltpu.SemaphoreType.DMA((2, CHAN)),
+        pltpu.SemaphoreType.DMA((2, CHAN)),
+        pltpu.SemaphoreType.REGULAR((2,)),
         pltpu.SemaphoreType.DMA((2,)),
     ]
 

time: 23 us -> 20.7 us (0.900)
  Pallas kernels: 22.2 us -> 19.9 us
    pallas_call x1, Pallas kernels: 22.2 us -> 19.9 us  [body(): pl.pallas_call(kernel, out_shape=jax.ShapeDtypeStruct(frames.shape, f32),...]
where the time goes in v3:
time: 20.7 us; the launch traced here: 20.6 us
  Pallas kernels  19.9 us (96%)
  local copies, waits for them, and re-layouts  0.73 us (4%)
    pallas_call x1, Pallas kernels, body(): pl.pallas_call(kernel, out_shape=jax.ShapeDtypeStruct(frames.shape, f32),...  19.9 us
    unnamed x1, local copies, waits for them, and re-layouts  0.73 us

profile of v3, /device:TPU:14, one launch (start us, length us, event | category | flops | bytes accessed | tf_op | source)
XLA Modules:
  0.0 20.6 jit_solution(6194287797444691323)
XLA Ops:
  0.0 19.9 %shard_map.172 = f32[1,320,256]{2,1,0:T(8,128)S(1)} custom-call(bf16[1,320,256]{2,1,0:T(8,128)(2,1)} %refs_0_.1, bf16[256,256]{1,0:T(8,128)(2,1)} %constant.22.clone.refs_1_, s32[1,2560]{1,0:T(1,128)} %refs_2_.1, f32[2,16,2816]{2,1,0:T(8,128)} %refs_3_.1, f32[1,128]{1,0:T(1,128)} %bitcast.4, f32[1,128]{1,0:T(1,128)} %bitcast.5, s32[1,4,20]{2,1,0:T(4,128)} %bitcast.3, ...), custom_call_target="tpu_custom_call" | custom-call | tf_op jit(solution)/shard_map/pallas_call | solution.py:587
  19.9 0.7 %copy.20 = f32[1,320,256]{2,1,0:T(8,128)} copy(f32[1,320,256]{2,1,0:T(8,128)S(1)} %shard_map.172) | data formatting | bytes 655360

commit v4 on v3

--- a/solution.py
+++ b/solution.py
@@ -28,6 +28,8 @@
 PE = PW + 2 * HALO
 NW = PE // RADIX
 OUTS = SHARE // RADIX
+HEAD = 256
+TAIL = CHANNELS // RADIX - HEAD
 
 MESH = pl.DeviceIdType.MESH
 NT = (((1,), (1,)), ((), ()))
@@ -57,7 +59,7 @@
     k, z = tick_rows()
     angle = 2.0 * math.pi / TICKS * (k[:, None] * np.arange(TICKS)[None, :] % TICKS)
     weight = np.where(k == 0, 1.0, 2.0)[:, None] / TICKS
-    return np.stack(halves(np.where(z[:, None] == 0, np.cos(angle), -np.sin(angle)) * weight))
+    return (np.where(z[:, None] == 0, np.cos(angle), -np.sin(angle)) * weight).astype(np.float32)
 
 
 def spread_filters():
@@ -74,9 +76,17 @@
     return table
 
 
-def forward_dense(length, width):
-    high, low = halves(dense(length, width))
+def forward_dense(length, width, places):
+    rows = dense(length, width)[np.maximum(places, 0)] * (places[:, None] >= 0)
+    high, low = halves(rows)
     return np.concatenate([high, high, low], axis=0)
+
+
+def lanes_of(lanes, *runs):
+    places = np.full(lanes, -1)
+    for lane, first, count in runs:
+        places[lane : lane + count] = first + np.arange(count)
+    return places
 
 
 def inverse_dense(length, width, period, first, count, lead, rows):
@@ -93,10 +103,10 @@
     return table
 
 
-def rim_places():
+def rim_table():
     lane = np.arange(2 * HALO)
-    place = np.where(lane < HALO, lane // RADIX, (HALO + PW) // RADIX + (lane - HALO) // RADIX)
-    return (np.arange(256)[:, None] == place[None, :]).astype(np.float32).astype(bf16)
+    places = np.where(lane < HALO, lane // RADIX, (PW + HALO) // RADIX + (lane - HALO) // RADIX)
+    return forward_dense(NW, 256, places)
 
 
 def levels_of(largest):
@@ -151,12 +161,13 @@
 
 
 def channel_product(product, kern, twiddle, width):
+    cosine, sine = product
     values = []
     for c in range(RADIX):
-        re = product[c * ROWS : c * ROWS + KB]
-        im = product[c * ROWS + KB : (c + 1) * ROWS]
-        yr = re[:, :width] + im[:, width:]
-        yi = im[:, :width] - re[:, width:]
+        re = slice(c * ROWS, c * ROWS + KB)
+        im = slice(c * ROWS + KB, (c + 1) * ROWS)
+        yr = cosine[re] + sine[im]
+        yi = cosine[im] - sine[re]
         if c > 0:
             tc, ts = twiddle[0, c], twiddle[1, c]
             yr, yi = yr * tc + yi * ts, yi * tc - yr * ts
@@ -197,7 +208,7 @@
     return piece[:, :width]
 
 
-INPUTS = 18
+INPUTS = 19
 LEVELS = 32000.0
 STEPS = 8.0
 
@@ -206,11 +217,11 @@
     hbm = refs[:INPUTS]
     out = refs[INPUTS]
     local = refs[INPUTS + 1 : 2 * INPUTS + 1]
-    (tx1, rx1, tx2, rx2, txh, rxh, onehot, masks, big, kern_u, kern_v, kern_w, result) = refs[
-        2 * INPUTS + 1 : 2 * INPUTS + 14
+    (tx1, rx1, tx2, rx2, txh, rxh, onehot, masks, big, inverse, kern_u, kern_v, kern_w, result) = refs[
+        2 * INPUTS + 1 : 2 * INPUTS + 15
     ]
-    in_sem, send1, recv1, send2, recv2, sendh, recvh, entered, out_sem = refs[2 * INPUTS + 14 :]
-    (frames, ticks, links, kern, wide, tight, roi, fwd_u, fwd_w, inv_u, inv_v, inv_w, tw_u, tw_w, rim, back, expand, near) = local
+    in_sem, send1, recv1, send2, recv2, sendh, recvh, entered, out_sem = refs[2 * INPUTS + 15 :]
+    (frames, ticks, links, near, kern, wide, tight, roi, fwd_u, fwd_w, inv_u, inv_v, inv_w, tw_u, tw_w, rim, back, expand, fwd_v) = local
 
     me = lax.axis_index("chan")
     apa = lax.axis_index("apa")
@@ -224,16 +235,40 @@
     greet_after = has_after & jnp.logical_not(wait_after)
     greet_before = has_before & jnp.logical_not(wait_before)
 
+    loads = [pltpu.make_async_copy(hbm[i], local[i], in_sem.at[i]) for i in range(INPUTS)]
+    for load in loads[:4]:
+        load.start()
     barrier = pltpu.get_barrier_semaphore()
     for step in range(1, CHAN):
         pl.semaphore_signal(barrier, inc=1, device_id={"chan": lax.rem(me + step, CHAN)}, device_id_type=MESH)
-    loads = [pltpu.make_async_copy(hbm[i], local[i], in_sem.at[i]) for i in range(INPUTS)]
-    for load in loads:
+    for load in loads[4:]:
         load.start()
+
+    loads[2].wait()
+    loads[3].wait()
+    mine = jnp.zeros((1, SHARE), jnp.int32)
+    for s in range(CHAN):
+        mine = jnp.where(me == s, links[:, s * SHARE : (s + 1) * SHARE], mine)
+    mine = jnp.concatenate([mine, jnp.full((1, PAD - SHARE), -8, jnp.int32)], axis=1)
+    row = lax.broadcasted_iota(jnp.int32, (2 * HALO, PAD), 0)
+    spot = row + jnp.where(row >= HALO, CHANNELS - 2 * HALO, PU + PV)
+    local_edge = jnp.where(spot == mine, 1.0, 0.0).astype(bf16)
 
     loads[0].wait()
     loads[1].wait()
     padded = jnp.concatenate([frames[0], jnp.zeros((PAD - SHARE, TICKS), bf16)], axis=0)
+    bands = mul_nt(ticks[...], mul(local_edge, padded).astype(bf16))
+    first_band = bands[:, :HALO]
+    last_band = bands[:, HALO:]
+    lower = jnp.broadcast_to(near[:, 0:1], first_band.shape)
+    upper = jnp.broadcast_to(near[:, 1:2], first_band.shape)
+    none = jnp.zeros_like(first_band)
+    to_after = jnp.where(upper == after, last_band, jnp.where(lower == after, first_band, none))
+    to_before = jnp.where(lower == before, first_band, jnp.where(upper == before, last_band, none))
+    for way, band in enumerate([to_after, to_before]):
+        for dest in range(CHAN):
+            txh[way, dest] = message(band[dest * ROWS : (dest + 1) * ROWS])
+
     spectra = mul_nt(ticks[...], padded)
     level = levels_of(jnp.max(jnp.abs(spectra), axis=1, keepdims=True))
     scaled = jnp.round(spectra * (LEVELS * jnp.exp2(-level / STEPS)))
@@ -249,6 +284,32 @@
     @pl.when(greet_before)
     def _():
         pl.semaphore_signal(barrier, inc=1, device_id={"apa": before}, device_id_type=MESH)
+
+    @pl.when(wait_after)
+    def _():
+        pl.semaphore_signal(entered.at[1], inc=1, device_id={"apa": after}, device_id_type=MESH)
+
+    @pl.when(wait_before)
+    def _():
+        pl.semaphore_signal(entered.at[0], inc=1, device_id={"apa": before}, device_id_type=MESH)
+
+    def edge_copy(way, dest):
+        return pltpu.make_async_remote_copy(
+            src_ref=txh.at[way, dest],
+            dst_ref=rxh.at[way, me],
+            send_sem=sendh.at[way, dest],
+            recv_sem=recvh.at[way, me],
+            device_id={"apa": after if way == 0 else before, "chan": dest},
+            device_id_type=MESH,
+        )
+
+    def send_edges(way):
+        for step in range(CHAN):
+            edge_copy(way, lax.rem(me + step, CHAN)).start()
+
+    @pl.when(wait_after & (after == apas // 2))
+    def _():
+        send_edges(0)
 
     def first_copy(step):
         dest = lax.rem(me + step, CHAN)
@@ -265,51 +326,7 @@
         first_copy(step).start()
     rx1[me] = tx1[me]
 
-    @pl.when(wait_after)
-    def _():
-        pl.semaphore_signal(entered.at[1], inc=1, device_id={"apa": after}, device_id_type=MESH)
-
-    @pl.when(wait_before)
-    def _():
-        pl.semaphore_signal(entered.at[0], inc=1, device_id={"apa": before}, device_id_type=MESH)
-
-    loads[2].wait()
-    loads[17].wait()
-    mine = jnp.zeros((1, SHARE), jnp.int32)
-    for s in range(CHAN):
-        mine = jnp.where(me == s, links[:, s * SHARE : (s + 1) * SHARE], mine)
-    mine = jnp.concatenate([mine, jnp.full((1, PAD - SHARE), -8, jnp.int32)], axis=1)
-    row = lax.broadcasted_iota(jnp.int32, (2 * HALO, PAD), 0)
-    spot = row + jnp.where(row >= HALO, CHANNELS - 2 * HALO, PU + PV)
-    local_edge = jnp.where(spot == mine, 1.0, 0.0).astype(bf16)
-    high, low = split(spectra)
-    bands = mul_nt(high, local_edge) + mul_nt(low, local_edge)
-    first_band = bands[:, :HALO]
-    last_band = bands[:, HALO:]
-    lower = jnp.broadcast_to(near[:, 0:1], first_band.shape)
-    upper = jnp.broadcast_to(near[:, 1:2], first_band.shape)
-    none = jnp.zeros_like(first_band)
-    to_after = jnp.where(upper == after, last_band, jnp.where(lower == after, first_band, none))
-    to_before = jnp.where(lower == before, first_band, jnp.where(upper == before, last_band, none))
-    for way, band in enumerate([to_after, to_before]):
-        for dest in range(CHAN):
-            txh[way, dest] = message(band[dest * ROWS : (dest + 1) * ROWS])
-
-    def edge_copy(way, dest):
-        return pltpu.make_async_remote_copy(
-            src_ref=txh.at[way, dest],
-            dst_ref=rxh.at[way, me],
-            send_sem=sendh.at[way, dest],
-            recv_sem=recvh.at[way, me],
-            device_id={"apa": after if way == 0 else before, "chan": dest},
-            device_id_type=MESH,
-        )
-
-    def send_edges(way):
-        for step in range(CHAN):
-            edge_copy(way, lax.rem(me + step, CHAN)).start()
-
-    @pl.when(wait_after)
+    @pl.when(wait_after & (after != apas // 2))
     def _():
         send_edges(0)
 
@@ -330,23 +347,35 @@
         wire = links[:, lanes]
         group = lax.shift_right_arithmetic(wire, 3)
         rest = lax.bitwise_and(wire, 7)
-        place = group + jnp.where(wire >= PU + PV, 72, jnp.where(wire >= PU, 28, 0))
-        row = lax.broadcasted_iota(jnp.int32, (512, 512), 0)
-        onehot[:, lanes] = jnp.where(row == place, 1.0, 0.0).astype(bf16)
+        other = lax.shift_right_arithmetic(rest, 1) * TAIL + group - HEAD
+        other = jnp.where(group >= HEAD, other, -1)
+        row = lax.broadcasted_iota(jnp.int32, (256, 512), 0)
+        onehot[0:256, lanes] = jnp.where(row == group, 1.0, 0.0).astype(bf16)
+        onehot[256:512, lanes] = jnp.where(row == other, 1.0, 0.0).astype(bf16)
         for h in range(RADIX):
             masks[h, :, lanes] = jnp.broadcast_to(jnp.where(rest == h, 1.0, 0.0), (16, 512)).astype(bf16)
-
-    loads[3].wait()
+        parity = lax.bitwise_and(wire, 1)
+        for h in range(2):
+            masks[RADIX + h, :, lanes] = jnp.broadcast_to(jnp.where(parity == h, 1.0, 0.0), (16, 512)).astype(bf16)
+
+    loads[4].wait()
     for m in range(RADIX):
         for part in range(2):
             kern_u[m, part] = kernel_window(kern, part, NU * m, NU, 128)
             kern_v[m, part] = kernel_window(kern, part, PU + NU * m, NU, 128)
             kern_w[m, part] = kernel_window(kern, part, PU + PV + NW * m, NW, 256)
 
-    for load in loads[4:17]:
+    for load in loads[5:]:
         load.wait()
     gains = jnp.concatenate([wide[...], tight[...], jnp.zeros((6, FREQS), f32)], axis=0)
     gains = jnp.dot(gains, expand[0:FREQS], precision=lax.Precision.HIGHEST, preferred_element_type=f32)
+    gains = jnp.transpose(gains)
+    for column in range(2):
+        high, low = split(back[...] * gains[:, column : column + 1])
+        lanes = slice(column * TICKS, (column + 1) * TICKS)
+        inverse[0:256, lanes] = high
+        inverse[256:512, lanes] = high
+        inverse[512:768, lanes] = low
     inside = roi[0].astype(f32)
     row_index = lax.broadcasted_iota(jnp.int32, (OUTS, SHARE // BC), 0) // (BC // RADIX)
     col_index = lax.broadcasted_iota(jnp.int32, (OUTS, SHARE // BC), 1)
@@ -361,7 +390,7 @@
         pl.semaphore_wait(entered.at[0], 1)
         send_edges(0)
 
-    @pl.when(greet_before)
+    @pl.when(greet_before & jnp.logical_not(even))
     def _():
         pl.semaphore_wait(entered.at[1], 1)
         send_edges(1)
@@ -376,6 +405,11 @@
             device_id={"chan": source},
             device_id_type=MESH,
         ).wait_recv()
+    @pl.when(greet_before & even)
+    def _():
+        pl.semaphore_wait(entered.at[1], 1)
+        send_edges(1)
+
     for pair in range(CHAN // 2):
         lanes = slice(pair * 2 * SHARE, (pair + 1) * 2 * SHARE)
         values = []
@@ -383,11 +417,13 @@
             value = from_short(rx1[s])
             values.append(value[:, :SHARE] * (jnp.exp2(value[:, SHARE : SHARE + 1] / STEPS) / LEVELS))
         high, low = split(jnp.concatenate(values, axis=1))
-        for h in range(RADIX):
+        for h in range(RADIX + 2):
             mask = jnp.concatenate([masks[h, :, lanes], masks[h, :, lanes]], axis=0)
-            big[h * ROWS : (h + 1) * ROWS, lanes] = high * mask
-            big[256 + h * ROWS : 256 + (h + 1) * ROWS, lanes] = low * mask
-    placed = mul_nt(big[...], onehot[...])
+            first = h * ROWS if h < RADIX else 512 + (h - RADIX) * ROWS
+            second = first + (256 if h < RADIX else 2 * ROWS)
+            big[first : first + ROWS, lanes] = high * mask
+            big[second : second + ROWS, lanes] = low * mask
+    placed = [mul_nt(big[0:256], onehot[0:256]), mul_nt(big[256:512], onehot[0:256])]
 
     def second_copy(dest):
         return pltpu.make_async_remote_copy(
@@ -410,18 +446,35 @@
             def _():
                 rx2[dest] = tx2[dest]
 
-    def plane(lanes, fwd, kern_part, twiddle, table, width):
-        high = placed[0:256, lanes].astype(bf16)
-        low = placed[256:512, lanes].astype(bf16)
-        product = mul(jnp.concatenate([high, low, high], axis=1), fwd[...])
-        return inverse_product(table, channel_product(product, kern_part, twiddle, width))
-
-    part_u = plane(slice(0, 128), fwd_u, kern_u, tw_u, inv_u, 128)
-    part_v = plane(slice(128, 256), fwd_u, kern_v, tw_u, inv_v, 128)
+    def first_stage(lanes, fwd, width):
+        high = placed[0][:, lanes].astype(bf16)
+        low = placed[1][:, lanes].astype(bf16)
+        value = jnp.concatenate([high, low, high], axis=1)
+        both = mul(value, fwd[...])
+        return both[:, :width], both[:, width:]
+
+    stage_u = first_stage(slice(0, 128), fwd_u, 128)
+    stage_v = first_stage(slice(0, 256), fwd_v, 128)
+    tail = mul_nt(big[512:640], onehot[256:512])
+    part_u = inverse_product(inv_u, channel_product(stage_u, kern_u, tw_u, 128))
+    part_v = inverse_product(inv_v, channel_product(stage_v, kern_v, tw_u, 128))
     middle = jnp.concatenate([part_u[80:96], part_u[96:104] + part_v[0:8], part_v[8:24]], axis=0)
     for dest, part in enumerate([part_u[0:40], part_u[40:80], middle, part_v[24:64], part_v[64:104]]):
         tx2[dest] = message(part)
     send_on(range(0, 5))
+
+    ends = []
+    for part in range(2):
+        for c in range(RADIX):
+            pair = c // 2
+            first = part * 2 * ROWS + c % 2 * ROWS
+            piece = tail[first : first + ROWS, pair // 2 * 128 : (pair // 2 + 1) * 128]
+            if pair % 2:
+                piece = pltpu.roll(piece, TAIL, axis=1)
+            ends.append(piece)
+    high = jnp.concatenate([placed[0][:, 128:256], jnp.concatenate(ends[:RADIX], axis=0)], axis=1).astype(bf16)
+    low = jnp.concatenate([placed[1][:, 128:256], jnp.concatenate(ends[RADIX:], axis=0)], axis=1).astype(bf16)
+    native = mul(jnp.concatenate([high, low, high], axis=1), fwd_w[...])
 
     def edge_arrivals(way):
         for source in range(CHAN):
@@ -457,12 +510,12 @@
     rim_up = jnp.where(upper == after, from_after, jnp.where(upper == before, from_before, blank))
     rims = jnp.concatenate([rim_low, rim_up], axis=1)
     lane = lax.bitwise_and(lax.broadcasted_iota(jnp.int32, (ROWS, 2 * HALO), 1), RADIX - 1)
-    spread = [jnp.where(lane == h, part.astype(f32), 0.0) for part in split(rims) for h in range(RADIX)]
-    rim_part = mul_nt(jnp.concatenate(spread, axis=0).astype(bf16), rim[...])
-    full = placed[:, 256:512] + rim_part
-    high = full[0:256].astype(bf16)
-    low = full[256:512].astype(bf16)
-    product = mul(jnp.concatenate([high, low, high], axis=1), fwd_w[...])
+    spread = [
+        jnp.concatenate([jnp.where(lane == h, part.astype(f32), 0.0) for h in range(RADIX)], axis=0).astype(bf16)
+        for part in split(rims)
+    ]
+    added = mul(jnp.concatenate([spread[0], spread[1], spread[0]], axis=1), rim[...])
+    product = native[:, :256] + added[:, :256], native[:, 256:] + added[:, 256:]
     part_w = inverse_product(inv_w, channel_product(product, kern_w, tw_w, 256))
     for dest in range(3):
         tx2[5 + dest] = message(part_w[dest * OUTS : (dest + 1) * OUTS])
@@ -499,15 +552,11 @@
         [jnp.concatenate(columns[:RADIX], axis=0), jnp.concatenate(columns[RADIX:], axis=0)], axis=1
     )
 
-    def signal(gain):
-        high, low = split(gathered * gain)
-        return mul(high, back[0]) + mul(low, back[0]) + mul(high, back[1])
-
-    wide_signal = signal(gains[0:1])
-    tight_signal = signal(gains[1:2])
+    high, low = split(gathered)
+    signals = mul(jnp.concatenate([high, low, high], axis=1), inverse[...])
     for c in range(RADIX):
         rows = slice(c * OUTS, (c + 1) * OUTS)
-        chosen = jnp.where(inside > 0.5, wide_signal[rows], tight_signal[rows])
+        chosen = jnp.where(inside > 0.5, signals[rows, :TICKS], signals[rows, TICKS:])
         for side in range(2):
             result[side, pl.ds(c, OUTS, stride=RADIX), :] = chosen[:, side * 128 : (side + 1) * 128]
     stores = [
@@ -535,25 +584,29 @@
 
 def body(frames, links, near, kern, wide, tight, roi):
     apas = lax.axis_size("apa")
+    rim = HALO // RADIX
+    head = HEAD - 2 * NU
+    collection = ((128 - head, rim, head), (128, rim + head, TAIL))
     arrays = [
         frames,
         jnp.asarray(forward_ticks()),
         links,
+        near,
         kern,
         wide.reshape(1, FREQS),
         tight.reshape(1, FREQS),
         jnp.swapaxes(roi, 1, 2),
-        jnp.asarray(forward_dense(NU, 128)),
-        jnp.asarray(forward_dense(NW, 256)),
+        jnp.asarray(forward_dense(NU, 128, lanes_of(128, (0, 0, NU)))),
+        jnp.asarray(forward_dense(NW, 256, lanes_of(256, *collection))),
         jnp.asarray(inverse_dense(NU, 128, PU, 0, NU, 0, 104)),
         jnp.asarray(inverse_dense(NU, 128, PV, 0, NU, 4, 104)),
         jnp.asarray(inverse_dense(NW, 256, PE, HALO // RADIX, PW // RADIX, 0, 120)),
         jnp.asarray(twiddles(NU, 128, PU)),
         jnp.asarray(twiddles(NW, 256, PE)),
-        jnp.asarray(rim_places()),
+        jnp.asarray(rim_table()),
         jnp.asarray(inverse_ticks()),
         jnp.asarray(spread_filters()),
-        near,
+        jnp.asarray(forward_dense(NU, 128, lanes_of(256, (NU, 0, NU)))),
     ]
     scratch = [pltpu.VMEM(a.shape, a.dtype) for a in arrays]
     scratch += [
@@ -564,8 +617,9 @@
         pltpu.VMEM((2, CHAN, ROWS + 8, HALO), jnp.int16),
         pltpu.VMEM((2, CHAN, ROWS + 8, HALO), jnp.int16),
         pltpu.VMEM((512, CHANNELS), bf16),
-        pltpu.VMEM((RADIX, 16, CHANNELS), bf16),
-        pltpu.VMEM((512, CHANNELS), bf16),
+        pltpu.VMEM((RADIX + 2, 16, CHANNELS), bf16),
+        pltpu.VMEM((640, CHANNELS), bf16),
+        pltpu.VMEM((768, 2 * TICKS), bf16),
         pltpu.VMEM((RADIX, 2, KB, 128), f32),
         pltpu.VMEM((RADIX, 2, KB, 128), f32),
         pltpu.VMEM((RADIX, 2, KB, 256), f32),

time: 20.7 us -> 19.4 us (0.937)
  Pallas kernels: 19.9 us -> 18.4 us
    pallas_call x1, Pallas kernels: 19.9 us -> 18.4 us  [body(): pl.pallas_call(kernel, out_shape=jax.ShapeDtypeStruct(frames.shape, f32),...]
where the time goes in v4:
time: 19.4 us; the launch traced here: 19.2 us
  Pallas kernels  18.4 us (95%)
  local copies, waits for them, and re-layouts  0.73 us (4%)
    pallas_call x1, Pallas kernels, body(): pl.pallas_call(kernel, out_shape=jax.ShapeDtypeStruct(frames.shape, f32),...  18.4 us
    unnamed x1, local copies, waits for them, and re-layouts  0.73 us

profile of v4, /device:TPU:14, one launch (start us, length us, event | category | flops | bytes accessed | tf_op | source)
XLA Modules:
  0.0 19.2 jit_solution(7733556963757021043)
XLA Ops:
  0.0 18.4 %shard_map.181 = f32[1,320,256]{2,1,0:T(8,128)S(1)} custom-call(bf16[1,320,256]{2,1,0:T(8,128)(2,1)} %refs_0_.1, bf16[256,256]{1,0:T(8,128)(2,1)} %constant.24.clone.refs_1_, s32[1,2560]{1,0:T(1,128)} %refs_2_.1, s32[1,2]{1,0:T(1,128)} %refs_3_.1, f32[2,16,2816]{2,1,0:T(8,128)} %refs_4_.1, f32[1,128]{1,0:T(1,128)} %bitcast.4, f32[1,128]{1,0:T(1,128)} %bitcast.5, ...), custom_call_target="tpu_custom_call" | custom-call | tf_op jit(solution)/shard_map/pallas_call | solution.py:641
  18.5 0.7 %copy.21 = f32[1,320,256]{2,1,0:T(8,128)} copy(f32[1,320,256]{2,1,0:T(8,128)S(1)} %shard_map.181) | data formatting | bytes 655360

commit v5 on v4

--- a/solution.py
+++ b/solution.py
@@ -28,6 +28,8 @@
 PE = PW + 2 * HALO
 NW = PE // RADIX
 OUTS = SHARE // RADIX
+SIDE = 4
+FAR_FIRST = ((1, 2), (1, 3), (1, 1), (0, 2), (0, 3), (0, 1), (1, 0))
 HEAD = 256
 TAIL = CHANNELS // RADIX - HEAD
 
@@ -235,6 +237,10 @@
     greet_after = has_after & jnp.logical_not(wait_after)
     greet_before = has_before & jnp.logical_not(wait_before)
 
+    def partner(step):
+        across, along = FAR_FIRST[step - 1]
+        return lax.rem(me // SIDE + across, CHAN // SIDE) * SIDE + lax.rem(me % SIDE + along, SIDE)
+
     loads = [pltpu.make_async_copy(hbm[i], local[i], in_sem.at[i]) for i in range(INPUTS)]
     for load in loads[:4]:
         load.start()
@@ -304,15 +310,16 @@
         )
 
     def send_edges(way):
-        for step in range(CHAN):
-            edge_copy(way, lax.rem(me + step, CHAN)).start()
+        for step in range(1, CHAN):
+            edge_copy(way, partner(step)).start()
+        edge_copy(way, me).start()
 
     @pl.when(wait_after & (after == apas // 2))
     def _():
         send_edges(0)
 
     def first_copy(step):
-        dest = lax.rem(me + step, CHAN)
+        dest = partner(step)
         return pltpu.make_async_remote_copy(
             src_ref=tx1.at[dest],
             dst_ref=rx1.at[me],
@@ -435,16 +442,17 @@
             device_id_type=MESH,
         )
 
-    def send_on(dests):
-        for dest in dests:
-
-            @pl.when(me != dest)
+    def send_on(chosen):
+        for step in range(1, CHAN):
+            dest = partner(step)
+
+            @pl.when(chosen(dest))
             def _():
                 second_copy(dest).start()
 
-            @pl.when(me == dest)
-            def _():
-                rx2[dest] = tx2[dest]
+        @pl.when(chosen(me))
+        def _():
+            rx2[me] = tx2[me]
 
     def first_stage(lanes, fwd, width):
         high = placed[0][:, lanes].astype(bf16)
@@ -461,7 +469,7 @@
     middle = jnp.concatenate([part_u[80:96], part_u[96:104] + part_v[0:8], part_v[8:24]], axis=0)
     for dest, part in enumerate([part_u[0:40], part_u[40:80], middle, part_v[24:64], part_v[64:104]]):
         tx2[dest] = message(part)
-    send_on(range(0, 5))
+    send_on(lambda dest: dest < 5)
 
     ends = []
     for part in range(2):
@@ -519,7 +527,7 @@
     part_w = inverse_product(inv_w, channel_product(product, kern_w, tw_w, 256))
     for dest in range(3):
         tx2[5 + dest] = message(part_w[dest * OUTS : (dest + 1) * OUTS])
-    send_on(range(5, 8))
+    send_on(lambda dest: dest >= 5)
 
     for step in range(1, CHAN):
         source = lax.rem(me + step, CHAN)

time: 19.4 us -> 19.1 us (0.985)
  no operation moved by 1% of the time
where the time goes in v5:
time: 19.1 us; the launch traced here: 19 us
  Pallas kernels  18.3 us (96%)
  local copies, waits for them, and re-layouts  0.73 us (4%)
    pallas_call x1, Pallas kernels, body(): pl.pallas_call(kernel, out_shape=jax.ShapeDtypeStruct(frames.shape, f32),...  18.3 us
    unnamed x1, local copies, waits for them, and re-layouts  0.73 us

profile of v5, /device:TPU:14, one launch (start us, length us, event | category | flops | bytes accessed | tf_op | source)
XLA Modules:
  0.0 19.0 jit_solution(2295385583479497151)
XLA Ops:
  0.0 18.3 %shard_map.181 = f32[1,320,256]{2,1,0:T(8,128)S(1)} custom-call(bf16[1,320,256]{2,1,0:T(8,128)(2,1)} %refs_0_.1, bf16[256,256]{1,0:T(8,128)(2,1)} %constant.24.clone.refs_1_, s32[1,2560]{1,0:T(1,128)} %refs_2_.1, s32[1,2]{1,0:T(1,128)} %refs_3_.1, f32[2,16,2816]{2,1,0:T(8,128)} %refs_4_.1, f32[1,128]{1,0:T(1,128)} %bitcast.4, f32[1,128]{1,0:T(1,128)} %bitcast.5, ...), custom_call_target="tpu_custom_call" | custom-call | tf_op jit(solution)/shard_map/pallas_call | solution.py:649
  18.3 0.7 %copy.21 = f32[1,320,256]{2,1,0:T(8,128)} copy(f32[1,320,256]{2,1,0:T(8,128)S(1)} %shard_map.181) | data formatting | bytes 655360

commit v6 on v5

--- a/solution.py
+++ b/solution.py
@@ -191,7 +191,13 @@
 
 def inverse_product(table, value):
     high, low = split(value)
-    return mul_nt(table[0], high) + mul_nt(table[1], high) + mul_nt(table[0], low)
+    if table.shape[1] == 104:
+        return mul_nt(table[0], high) + mul_nt(table[1], high) + mul_nt(table[0], low)
+    parts = []
+    for rows in (slice(0, 64), slice(64, table.shape[1])):
+        first, second = table[0, rows], table[1, rows]
+        parts.append(mul_nt(first, high) + mul_nt(second, high) + mul_nt(first, low))
+    return jnp.concatenate(parts, axis=0)
 
 
 def message(part):
@@ -247,8 +253,6 @@
     barrier = pltpu.get_barrier_semaphore()
     for step in range(1, CHAN):
         pl.semaphore_signal(barrier, inc=1, device_id={"chan": lax.rem(me + step, CHAN)}, device_id_type=MESH)
-    for load in loads[4:]:
-        load.start()
 
     loads[2].wait()
     loads[3].wait()
@@ -331,6 +335,8 @@
 
     for step in range(1, CHAN):
         first_copy(step).start()
+    for load in loads[4:]:
+        load.start()
     rx1[me] = tx1[me]
 
     @pl.when(wait_after & (after != apas // 2))
@@ -482,7 +488,8 @@
             ends.append(piece)
     high = jnp.concatenate([placed[0][:, 128:256], jnp.concatenate(ends[:RADIX], axis=0)], axis=1).astype(bf16)
     low = jnp.concatenate([placed[1][:, 128:256], jnp.concatenate(ends[RADIX:], axis=0)], axis=1).astype(bf16)
-    native = mul(jnp.concatenate([high, low, high], axis=1), fwd_w[...])
+    operand = jnp.concatenate([high, low, high], axis=1)
+    native = jnp.concatenate([mul(operand[:128], fwd_w[...]), mul(operand[128:], fwd_w[...])], axis=0)
 
     def edge_arrivals(way):
         for source in range(CHAN):
@@ -522,7 +529,8 @@
         jnp.concatenate([jnp.where(lane == h, part.astype(f32), 0.0) for h in range(RADIX)], axis=0).astype(bf16)
         for part in split(rims)
     ]
-    added = mul(jnp.concatenate([spread[0], spread[1], spread[0]], axis=1), rim[...])
+    operand = jnp.concatenate([spread[0], spread[1], spread[0]], axis=1)
+    added = jnp.concatenate([mul(operand[:128], rim[...]), mul(operand[128:], rim[...])], axis=0)
     product = native[:, :256] + added[:, :256], native[:, 256:] + added[:, 256:]
     part_w = inverse_product(inv_w, channel_product(product, kern_w, tw_w, 256))
     for dest in range(3):

time: 19.1 us -> 18.9 us (0.990)
  Pallas kernels: 18.3 us -> 18.1 us
    pallas_call x1, Pallas kernels: 18.3 us -> 18.1 us  [body(): pl.pallas_call(kernel, out_shape=jax.ShapeDtypeStruct(frames.shape, f32),...]
where the time goes in v6:
time: 18.9 us; the launch traced here: 18.8 us
  Pallas kernels  18.1 us (96%)
  local copies, waits for them, and re-layouts  0.73 us (4%)
    pallas_call x1, Pallas kernels, body(): pl.pallas_call(kernel, out_shape=jax.ShapeDtypeStruct(frames.shape, f32),...  18.1 us
    unnamed x1, local copies, waits for them, and re-layouts  0.73 us

profile of v6, /device:TPU:14, one launch (start us, length us, event | category | flops | bytes accessed | tf_op | source)
XLA Modules:
  0.0 18.8 jit_solution(11581061138623671765)
XLA Ops:
  0.0 18.1 %shard_map.181 = f32[1,320,256]{2,1,0:T(8,128)S(1)} custom-call(bf16[1,320,256]{2,1,0:T(8,128)(2,1)} %refs_0_.1, bf16[256,256]{1,0:T(8,128)(2,1)} %constant.24.clone.refs_1_, s32[1,2560]{1,0:T(1,128)} %refs_2_.1, s32[1,2]{1,0:T(1,128)} %refs_3_.1, f32[2,16,2816]{2,1,0:T(8,128)} %refs_4_.1, f32[1,128]{1,0:T(1,128)} %bitcast.4, f32[1,128]{1,0:T(1,128)} %bitcast.5, ...), custom_call_target="tpu_custom_call" | custom-call | tf_op jit(solution)/shard_map/pallas_call | solution.py:657
  18.1 0.7 %copy.21 = f32[1,320,256]{2,1,0:T(8,128)} copy(f32[1,320,256]{2,1,0:T(8,128)S(1)} %shard_map.181) | data formatting | bytes 655360

commit v7 on v6

--- a/solution.py
+++ b/solution.py
@@ -581,8 +581,6 @@
     ]
     for store in stores:
         store.start()
-    for store in stores:
-        store.wait()
 
     for step in range(1, CHAN):
         first_copy(step).wait_send()
@@ -596,6 +594,9 @@
     def _():
         for dest in range(CHAN):
             edge_copy(1, dest).wait_send()
+
+    for store in stores:
+        store.wait()
 
 
 def body(frames, links, near, kern, wide, tight, roi):

time: 18.9 us -> 18.9 us (level)
  no operation moved by 1% of the time
where the time goes in v7:
time: 18.9 us; the launch traced here: 18.8 us
  Pallas kernels  18.1 us (96%)
  local copies, waits for them, and re-layouts  0.73 us (4%)
    pallas_call x1, Pallas kernels, body(): pl.pallas_call(kernel, out_shape=jax.ShapeDtypeStruct(frames.shape, f32),...  18.1 us
    unnamed x1, local copies, waits for them, and re-layouts  0.73 us

profile of v7, /device:TPU:14, one launch (start us, length us, event | category | flops | bytes accessed | tf_op | source)
XLA Modules:
  0.0 18.8 jit_solution(1333361880173213955)
XLA Ops:
  0.0 18.1 %shard_map.181 = f32[1,320,256]{2,1,0:T(8,128)S(1)} custom-call(bf16[1,320,256]{2,1,0:T(8,128)(2,1)} %refs_0_.1, bf16[256,256]{1,0:T(8,128)(2,1)} %constant.24.clone.refs_1_, s32[1,2560]{1,0:T(1,128)} %refs_2_.1, s32[1,2]{1,0:T(1,128)} %refs_3_.1, f32[2,16,2816]{2,1,0:T(8,128)} %refs_4_.1, f32[1,128]{1,0:T(1,128)} %bitcast.4, f32[1,128]{1,0:T(1,128)} %bitcast.5, ...), custom_call_target="tpu_custom_call" | custom-call | tf_op jit(solution)/shard_map/pallas_call | solution.py:658
  18.1 0.7 %copy.21 = f32[1,320,256]{2,1,0:T(8,128)} copy(f32[1,320,256]{2,1,0:T(8,128)S(1)} %shard_map.181) | data formatting | bytes 655360
